TPU v7x, 32 devices: a whole 2x2x4 slice. The times are simulated.
32 devices in a mesh: dp: 8 (over z, y), seq: 4 (over x, core).
Axes of the slice: x: 2, y: 2, z: 4, core: 2. Of those that a mesh axis runs over, the one named last changes fastest.
Arguments:
- inputs: float32 [8, 1024, 768], P('dp', 'seq'), may hold values from -40 to 40
- out_grad: float32 [8, 1024, 768], P('dp', 'seq'), may hold values from -6 to 6
- segment_ids: int32 [8, 1024], P('dp'), may hold values from 0 to 3, never falling along the last dimension, each value on 1 to 512 neighbouring positions
- params: float32 [3768320], P(('dp', 'seq')), may hold values from -7 to 2, as said below
- moment_one: float32 [3768320], P(('dp', 'seq')), may hold values from -28 to 28
- moment_two: float32 [3768320], P(('dp', 'seq')), may hold values from 40.96 to 409.6
Outputs:
- activations: float32 [8, 1024, 768], P('dp', 'seq')
- input_grad: float32 [8, 1024, 768], P('dp', 'seq')
- grad_flat: float32 [3768320], P(('dp', 'seq'))
- new_params: float32 [3768320], P(('dp', 'seq'))
- new_moment_one: float32 [3768320], P(('dp', 'seq'))
- new_moment_two: float32 [3768320], P(('dp', 'seq'))
Inputs may be any that keep to these rules, and one draw needn't show every extreme that they name: segment_ids number the documents of each packed sequence from 0; they never fall along a sequence, each document holds 1 to 512 tokens and one holds exactly 512. The entries of params after the first 3765320 are zero.
All inputs are finite; a program needn't handle non-finite values.
Results may differ from a plain program's by a relative error of at most 0.011.
The roundings to bfloat16 on the way count: a program that leaves them out, or rounds other values in their place, can miss the bound.
Values may be sent and summed in bfloat16 or wider, within the bound.
No kernel may reach another device: no remote copies, remote signals or barrier semaphores. Data moves between devices by JAX's collectives and lax.ppermute only.
A program may use at most 128 MiB of HBM per device.

v0:
```python
import functools

import jax
import jax.numpy as jnp
import numpy as np
from jax import lax
from jax.experimental import pallas as pl
from jax.experimental.pallas import tpu as pltpu
from jax.sharding import PartitionSpec as P

D = 768
HEADS = 24
HEAD_DIM = 64
STATE = 128
KERNEL = 4
INNER = 1536
PROJ = 3352

NORM_EPS = 1e-05
BETA_ONE = 0.9
BETA_TWO = 0.95
LEARN_RATE = 0.02
WEIGHT_DECAY = 0.1
ADAM_EPS = 1e-08
CORRECT_ONE = 1.0 - BETA_ONE**2
CORRECT_TWO = 1.0 - BETA_TWO**2

LANES = 128
CHUNK = 128
GROUP = 4
OWN = INNER // GROUP
OWN_SLABS = OWN // LANES
MIXED = OWN + 2 * STATE
WIDE = 2 * OWN + 2 * STATE + LANES
SLABS = WIDE // LANES
HEADS_OWN = HEADS // GROUP
IN_SIZE = D * PROJ
OUT_END = IN_SIZE + INNER * D
ROW_SLABS = 32
OUT_SLABS = D // LANES
FRAME = HEAD_DIM * OUT_SLABS
SMALL = 48
PAD = FRAME + 16
MIB = 1024 * 1024

F32 = jnp.float32
BF16 = jnp.bfloat16


def up(value, step):
    return -(-value // step) * step


class Plan:
    def __init__(self, dp, seq, length):
        self.dp, self.seq, self.length = dp, seq, length
        count = dp * seq
        self.count = count
        self.first_out = IN_SIZE // length
        assert seq == GROUP and dp % 2 == 0 and length % LANES == 0
        assert IN_SIZE % length and (count - 1) * length <= OUT_END
        start = [i * length for i in range(count)]
        rows = []
        for i in range(self.first_out + 1):
            first = start[i] // PROJ
            last = (min(start[i] + length, IN_SIZE) - 1) // PROJ
            rows.append((first, last - first + 1))
        self.pure = up(max(n for _, n in rows[:-1]), 16)
        self.edge = up(rows[-1][1], 16)
        self.most_rows = max(n for _, n in rows)
        edge_out = -(-(start[self.first_out] + length - IN_SIZE) // D)
        assert edge_out <= HEAD_DIM
        self.edge_out = up(edge_out, 8)
        self.edge_at = SLABS * self.edge
        self.small_row = (OUT_END - start[-1]) // LANES
        self.pads = [self.pure] * self.first_out + [self.edge]
        self.offsets = [int(v) for v in np.cumsum([0] + self.pads[:-1])]
        self.depth = int(sum(self.pads))
        row_map = np.full((1, self.depth), -1, np.int32)
        for (first, n), at in zip(rows, self.offsets):
            row_map[0, at : at + n] = np.arange(first, first + n)
        self.row_map = row_map
        place = np.zeros((count, GROUP), np.int32)
        for i in range(self.first_out, count):
            low = max(start[i] - IN_SIZE, 0) // D // HEAD_DIM
            high = (min(start[i] + length, OUT_END) - 1 - IN_SIZE) // D // HEAD_DIM
            assert high - low < GROUP
            for head in range(low, high + 1):
                place[i, head % GROUP] = head // GROUP
        self.place = place
        self.frame_rows = HEAD_DIM if length > D * HEAD_DIM else up(length // D + 2, 8)
        if self.frame_rows < HEAD_DIM:
            for i in range(self.first_out, count):
                for rank in range(GROUP):
                    begin = max(start[i] - IN_SIZE, 0) // D
                    head = self.place[i, rank] * GROUP + rank
                    self.place[i, rank] = self.place[i, rank] * HEAD_DIM + max(
                        begin - head * HEAD_DIM, 0
                    )
        else:
            self.place = self.place * HEAD_DIM
        self.frame = self.frame_rows * OUT_SLABS
        need = max(
            SLABS * self.pure, self.edge_at + OUT_SLABS * self.edge_out, self.frame + SMALL
        )
        self.block = up(need, 16)

    def scalars(self, index):
        begin = index * self.length
        first = begin // PROJ
        last = (jnp.minimum(begin + self.length, IN_SIZE) - 1) // PROJ
        form = jnp.where(index < self.first_out, 0, jnp.where(index == self.first_out, 1, 2))
        low = jnp.maximum(begin - IN_SIZE, 0) // D // HEAD_DIM
        high = (jnp.minimum(begin + self.length, OUT_END) - 1 - IN_SIZE) // D // HEAD_DIM
        values = [form, first * PROJ - begin, last - first + 1, index == self.count - 1]
        counts = []
        for rank in range(GROUP):
            head = low + (rank - low) % GROUP
            row = head * HEAD_DIM
            rows = HEAD_DIM
            if self.frame_rows < HEAD_DIM:
                top = jnp.maximum(begin - IN_SIZE, 0) // D
                bottom = (jnp.minimum(begin + self.length, OUT_END) - 1 - IN_SIZE) // D + 1
                rows = jnp.minimum(row + HEAD_DIM, bottom) - jnp.maximum(row, top)
                row = jnp.maximum(row, top)
            at = (IN_SIZE + row * D - begin) // LANES
            held = (head <= high) & (form > 0)
            values.append(jnp.where(held, at, -PAD))
            counts.append(jnp.where(held, rows * OUT_SLABS, 0))
        values += counts
        return jnp.stack([jnp.asarray(v, jnp.int32) for v in values])


def lane_iota(rows):
    return lax.broadcasted_iota(jnp.int32, (rows, LANES), 1)


def join_halves(first, second, rank):
    lane = lane_iota(first.shape[0])
    if rank % 2 == 0:
        return jnp.where(lane < 64, first, pltpu.roll(second, 64, 1))
    return jnp.where(lane < 64, pltpu.roll(first, 64, 1), second)


def own_slab(get, rank, slab):
    return join_halves(get(4 * slab + rank // 2), get(4 * slab + 2 + rank // 2), rank)


def whole_slab(get, slab):
    half = (slab // 2) % 2
    return join_halves(get((2 * slab) % 4, slab // 4), get((2 * slab + 1) % 4, slab // 4), half)


def pack_kernel(plan, sc, x_ref, out_ref, flat, rowbuf, frame, small):
    local = x_ref.shape[0]
    flat[...] = jnp.zeros_like(flat)
    flat[PAD : PAD + local, :] = x_ref[...]
    out_ref[...] = jnp.zeros_like(out_ref)
    lane = lane_iota(ROW_SLABS)
    form = sc[0]

    @pl.when(form < 2)
    def _():
        rowbuf[...] = jnp.zeros_like(rowbuf)

        def row(r, carry):
            at = sc[1] + r * PROJ + PAD * LANES
            sub, shift = at // LANES, at % LANES
            turn = (LANES - shift) % LANES
            near = pltpu.roll(flat[pl.ds(sub, ROW_SLABS), :], turn, 1)
            far = pltpu.roll(flat[pl.ds(sub + 1, ROW_SLABS), :], turn, 1)
            joined = jnp.where(lane < LANES - shift, near, far)
            rowbuf[pl.ds(pl.multiple_of(r * ROW_SLABS, ROW_SLABS), ROW_SLABS), :] = jnp.where(
                r < sc[2], joined, 0.0
            )
            return carry

        lax.fori_loop(0, plan.most_rows, row, 0)

    def weights(depth):
        def get(column):
            return rowbuf[pl.ds(column, depth, stride=ROW_SLABS), :]

        for rank in range(GROUP):
            slabs = [own_slab(get, rank, m) for m in range(OWN_SLABS)]
            slabs += [own_slab(lambda c: get(12 + c), rank, m) for m in range(OWN_SLABS)]
            slabs += [get(24), get(25), jnp.where(lane_iota(depth) < HEADS, get(26), 0.0)]
            for j, slab in enumerate(slabs):
                out_ref[rank, j * depth : (j + 1) * depth, :] = slab.astype(BF16)

    @pl.when(form == 0)
    def _():
        weights(plan.pure)

    @pl.when(form == 1)
    def _():
        weights(plan.edge)

    def frames(rows, base):
        for rank in range(GROUP):
            row = lax.broadcasted_iota(jnp.int32, (plan.frame, LANES), 0)
            frame[...] = jnp.where(
                row < sc[8 + rank], flat[pl.ds(sc[4 + rank] + PAD, plan.frame), :], 0.0
            )
            for j in range(OUT_SLABS):
                out_ref[rank, base + j * rows : base + (j + 1) * rows, :] = frame[
                    pl.ds(j, rows, stride=OUT_SLABS), :
                ].astype(BF16)

    @pl.when(form == 1)
    def _():
        frames(plan.edge_out, plan.edge_at)

    @pl.when(form == 2)
    def _():
        frames(plan.frame_rows, 0)

    @pl.when(sc[3] == 1)
    def _():
        base = PAD + plan.small_row

        def get(row):
            return flat[base + row : base + row + 1, :]

        small[...] = jnp.zeros_like(small)
        for rank in range(GROUP):
            at = 0
            for k in range(KERNEL + 1):
                for m in range(OWN_SLABS):
                    small[at : at + 1, :] = own_slab(lambda c: get(14 * k + c), rank, m)
                    at += 1
                for row in (12, 13):
                    small[at : at + 1, :] = get(14 * k + row)
                    at += 1
            for row in range(70, 76):
                small[at : at + 1, :] = get(row)
                at += 1
            for m in range(OWN_SLABS):
                small[at : at + 1, :] = own_slab(lambda c: get(76 + c), rank, m)
                at += 1
            small[at : at + 1, :] = get(88)
            out_ref[rank, plan.frame : plan.frame + SMALL, :] = small[...].astype(BF16)


def unpack_kernel(
    plan, sc, blk, par, one, two, grad_ref, par_ref, one_ref, two_ref, flat, rowbuf, frame
):
    local = par.shape[0]
    flat[...] = jnp.zeros_like(flat)
    lane = lane_iota(ROW_SLABS)
    form = sc[0]

    def total(at, rows):
        parts = [blk[rank, at : at + rows, :].astype(F32) for rank in range(GROUP)]
        return (parts[0] + parts[1]) + (parts[2] + parts[3])

    def weights(depth):
        rowbuf[...] = jnp.zeros_like(rowbuf)

        def get(base):
            def piece(rank, m):
                at = (base + m) * depth
                return blk[rank, at : at + depth, :].astype(F32)

            return piece

        for half in range(2):
            for j in range(12):
                rowbuf[pl.ds(12 * half + j, depth, stride=ROW_SLABS), :] = whole_slab(
                    get(OWN_SLABS * half), j
                )
        for j in range(3):
            rowbuf[pl.ds(24 + j, depth, stride=ROW_SLABS), :] = total((6 + j) * depth, depth)

    def rows():
        def row(r, carry):
            at = sc[1] + r * PROJ + PAD * LANES
            sub, shift = at // LANES, at % LANES
            value = rowbuf[pl.ds(pl.multiple_of(r * ROW_SLABS, ROW_SLABS), ROW_SLABS), :]
            value = pltpu.roll(jnp.where(r < sc[2], value, 0.0), shift, 1)
            flat[pl.ds(sub, ROW_SLABS), :] += jnp.where(lane >= shift, value, 0.0)
            flat[pl.ds(sub + 1, ROW_SLABS), :] += jnp.where(lane < shift, value, 0.0)
            return carry

        lax.fori_loop(0, plan.most_rows, row, 0)

    def frames(count, base):
        for rank in range(GROUP):
            frame[...] = jnp.zeros_like(frame)
            for j in range(OUT_SLABS):
                frame[pl.ds(j, count, stride=OUT_SLABS), :] = blk[
                    rank, base + j * count : base + (j + 1) * count, :
                ].astype(F32)
            row = lax.broadcasted_iota(jnp.int32, (plan.frame, LANES), 0)
            flat[pl.ds(sc[4 + rank] + PAD, plan.frame), :] += jnp.where(
                row < sc[8 + rank], frame[...], 0.0
            )

    @pl.when(form == 0)
    def _():
        weights(plan.pure)
        rows()

    @pl.when(form == 1)
    def _():
        frames(plan.edge_out, plan.edge_at)
        weights(plan.edge)
        rows()

    @pl.when(form == 2)
    def _():
        frames(plan.frame_rows, 0)

    @pl.when(sc[3] == 1)
    def _():
        base = PAD + plan.small_row
        rows = [blk[rank, plan.frame : plan.frame + SMALL, :].astype(F32) for rank in range(GROUP)]
        summed = (rows[0] + rows[1]) + (rows[2] + rows[3])

        def get(start):
            return lambda rank, m: rows[rank][start + m : start + m + 1]

        for k in range(KERNEL + 1):
            at = base + 14 * k
            for j in range(12):
                flat[at + j : at + j + 1, :] = whole_slab(get(5 * k), j)
            flat[at + 12 : at + 14, :] = summed[5 * k + 3 : 5 * k + 5]
        flat[base + 70 : base + 76, :] = summed[25:31]
        for j in range(12):
            flat[base + 76 + j : base + 77 + j, :] = whole_slab(get(31), j)
        flat[base + 88 : base + 89, :] = summed[34:35]

    grad = flat[PAD : PAD + local, :]
    new_one = BETA_ONE * one[...] + (1.0 - BETA_ONE) * grad
    new_two = BETA_TWO * two[...] + (1.0 - BETA_TWO) * grad * grad
    params = par[...]
    grad_ref[...] = grad
    one_ref[...] = new_one
    two_ref[...] = new_two
    par_ref[...] = params - LEARN_RATE * (
        new_one / CORRECT_ONE / (jnp.sqrt(new_two / CORRECT_TWO) + ADAM_EPS)
        + WEIGHT_DECAY * params
    )


def mm(a, b):
    return lax.dot_general(a, b, (((1,), (0,)), ((), ())), preferred_element_type=F32)


def mm_nt(a, b):
    return lax.dot_general(a, b, (((1,), (1,)), ((), ())), preferred_element_type=F32)


def mm_tn(a, b):
    return lax.dot_general(a, b, (((0,), (0,)), ((), ())), preferred_element_type=F32)


def thirds(value):
    high = value.astype(BF16)
    rest = value - high.astype(F32)
    middle = rest.astype(BF16)
    return high, middle, (rest - middle.astype(F32)).astype(BF16)


def expand(value):
    rows = value.shape[0]
    lane = lane_iota(rows)
    return jnp.concatenate(
        [
            jnp.where(lane < 64, value[:, 8 * m : 8 * m + 1], value[:, 8 * m + 4 : 8 * m + 5])
            for m in range(OWN_SLABS)
        ],
        axis=1,
    )


def head_sums(value):
    row = lax.broadcasted_iota(jnp.int32, (OWN, LANES), 0)
    col = lax.broadcasted_iota(jnp.int32, (OWN, LANES), 1)
    pick = (col == GROUP * (row // HEAD_DIM)).astype(BF16)
    high = value.astype(BF16)
    low = (value - high.astype(F32)).astype(BF16)
    return mm(high, pick) + mm(low, pick)


def small_rows(small, start, count):
    return jnp.concatenate([small[start + m : start + m + 1, :] for m in range(count)], axis=1)


class Small:
    def __init__(self, small, rank):
        self.taps = [small_rows(small, 5 * k, 5) for k in range(KERNEL)]
        self.conv_bias = small_rows(small, 20, 5)
        self.gated_gain = small_rows(small, 31, OWN_SLABS)
        vec = small[34:35, :]
        lane = lane_iota(1)
        self.heads = (lane % GROUP == 0) & (lane < HEADS)

        def pick(at):
            turned = pltpu.roll(vec, (2 * LANES - at - rank) % LANES, 1)
            return jnp.where(self.heads, turned, 0.0)

        self.delta_bias = pick(0)
        self.rate = jnp.where(self.heads, -jnp.exp(pick(HEADS)), 0.0)
        self.skip = expand(pick(2 * HEADS))


def triangle(lower):
    row = lax.broadcasted_iota(jnp.int32, (CHUNK, CHUNK), 0)
    col = lax.broadcasted_iota(jnp.int32, (CHUNK, CHUNK), 1)
    return (row >= col) if lower else (row <= col)


class Front:
    def __init__(self, c, rank, sm, xf, proj, tok, segr):
        at = pl.multiple_of(c * CHUNK, CHUNK)
        window = xf[pl.ds(at, CHUNK + 8), :]
        self.shifted = [window[8 - d : 8 - d + CHUNK] for d in range(KERNEL)]
        tk = tok[pl.ds(at, CHUNK), :]
        self.masks = [None] + [tk[:, d : d + 1] for d in range(1, KERNEL)]
        conv = sm.conv_bias + sm.taps[KERNEL - 1] * self.shifted[0]
        for d in range(1, KERNEL):
            conv = conv + sm.taps[KERNEL - 1 - d] * self.shifted[d] * self.masks[d]
        self.conv = conv
        self.conv_sig = jax.nn.sigmoid(conv)
        act = conv * self.conv_sig
        self.values = act[:, :OWN]
        self.b = act[:, OWN : OWN + STATE].astype(BF16)
        self.c = act[:, OWN + STATE :].astype(BF16)
        raw = proj[pl.ds(at, CHUNK), WIDE - LANES :].astype(F32)
        pre = pltpu.roll(raw, (LANES - rank) % LANES, 1) + sm.delta_bias
        self.pre = pre
        self.step = jnp.where(
            sm.heads, jnp.maximum(pre, 0.0) + jnp.log1p(jnp.exp(-jnp.abs(pre))), 0.0
        )
        log_decay = self.step * sm.rate
        lower = triangle(True)
        ones = lower.astype(BF16)
        high, middle, low = thirds(log_decay)
        sums = mm(ones, high) + (mm(ones, middle) + mm(ones, low))
        self.sums = sums
        self.sums_t = sums.T
        last = sums[CHUNK - 1 : CHUNK, :]
        self.allowed = (tk[:, 0:1] == segr[pl.ds(c, 1), :]) & lower
        self.step_wide = expand(self.step)
        self.scaled = self.values * self.step_wide
        self.scaled_n = self.scaled.astype(BF16)
        self.head_in = expand(jnp.exp(sums) * tk[:, 4:5])
        self.tail = expand(jnp.exp(last - sums) * tk[:, 5:6])
        self.carry = expand(jnp.exp(last) * tk[CHUNK - 1 : CHUNK, 6:7])
        self.tail_scaled = self.tail * self.scaled
        self.scores = mm_nt(self.c, self.b)
        gate = proj[pl.ds(at, CHUNK), :OWN].astype(F32)
        self.gate = gate
        self.gate_sig = jax.nn.sigmoid(gate)
        self.gate_act = gate * self.gate_sig

    def decay(self, k):
        gap = self.sums[:, 4 * k : 4 * k + 1] - self.sums_t[4 * k : 4 * k + 1, :]
        return jnp.exp(jnp.where(self.allowed, gap, -1e30))

    def head(self, value, k):
        return value[:, HEAD_DIM * k : HEAD_DIM * (k + 1)]


def fill_xf(xf, proj, tokens):
    xf[0:8, :] = jnp.zeros((8, MIXED), F32)
    xf[8 : 8 + tokens, :] = proj[:, OWN : OWN + MIXED].astype(F32)


def forward_kernel(plan, place, sc, row_map, tok, segr, *refs):
    dp = plan.dp
    x_in, c_in, w_in = refs[:4], refs[4:8], refs[8 : 8 + dp]
    refs = refs[8 + dp :]
    (proj, ssd, d_gated, states, sums_ref, w_sf, w_out, small_ref, spread, x_hat, cots) = refs[:11]
    xs, blocks, w_acc, xf, state, sem = refs[11:]
    tokens = xs.shape[0]
    piece = tokens // GROUP
    rank, group = sc[0], sc[1]
    line = dp // 2
    copies = []
    for j in range(dp):
        where = lax.rem(group // 2 + line - j // 2, line) * 2 + lax.rem(group + j % 2, 2)
        copies.append(pltpu.make_async_copy(w_in[j], blocks.at[where], sem.at[j]))
    for r in range(GROUP):
        at = pl.multiple_of((rank ^ r) * piece, piece)
        copies.append(pltpu.make_async_copy(x_in[r], xs.at[pl.ds(at, piece)], sem.at[dp + r]))
        copies.append(
            pltpu.make_async_copy(c_in[r], cots.at[pl.ds(at, piece)], sem.at[dp + GROUP + r])
        )
    for copy in copies:
        copy.start()
    for copy in copies:
        copy.wait()

    def rows_of(i, at, depth):
        for j in range(SLABS):
            w_sf[pl.ds(at, depth), j * LANES : (j + 1) * LANES] = blocks[
                i // GROUP, i % GROUP, j * depth : (j + 1) * depth, :
            ]

    def pure_rows(i, carry):
        rows_of(i, pl.multiple_of(i * plan.pure, plan.pure), plan.pure)
        return carry

    lax.fori_loop(0, plan.first_out, pure_rows, 0)
    rows_of(plan.first_out, plan.offsets[-1], plan.edge)
    w_acc[...] = jnp.zeros_like(w_acc)
    for i in range(plan.first_out, plan.count):
        rows, base = (plan.edge_out, plan.edge_at) if i == plan.first_out else (plan.frame_rows, 0)
        at = place[i * GROUP + rank]
        if plan.frame_rows == HEAD_DIM:
            at = pl.multiple_of(at, HEAD_DIM)
        for j in range(OUT_SLABS):
            w_acc[j, pl.ds(at, rows), :] += blocks[
                i // GROUP, i % GROUP, base + j * rows : base + (j + 1) * rows, :
            ].astype(F32)
    for j in range(OUT_SLABS):
        w_out[:, j * LANES : (j + 1) * LANES] = w_acc[j, 0:OWN, :].astype(BF16)
    small = blocks[dp - 1, GROUP - 1, plan.frame : plan.frame + SMALL, :].astype(F32)
    small_ref[...] = small
    sm = Small(small, rank)
    norm_gain = small_rows(small, 25, OUT_SLABS)
    chosen = (
        lax.broadcasted_iota(jnp.int32, (D, plan.depth), 0) == row_map[...]
    ).astype(BF16)

    def tile(t, carry):
        at = pl.ds(pl.multiple_of(t * 256, 256), 256)
        x = xs[at, :]
        scale = lax.rsqrt(jnp.sum(x * x, axis=1, keepdims=True) * (1.0 / D) + NORM_EPS)
        unit = x * scale
        x_hat[at, :] = unit.astype(BF16)
        wide = mm((unit * norm_gain).astype(BF16), chosen).astype(BF16)
        spread[at, :] = wide
        proj[at, :] = mm(wide, w_sf[...]).astype(BF16)
        d_gated[at, :] = mm_nt(cots[at, :], w_out[...])
        return carry

    lax.fori_loop(0, tokens // 256, tile, 0)
    fill_xf(xf, proj, tokens)
    state[...] = jnp.zeros_like(state)

    def chunk(c, carry):
        at = pl.ds(pl.multiple_of(c * CHUNK, CHUNK), CHUNK)
        f = Front(c, rank, sm, xf, proj, tok, segr)
        inner = []
        for k in range(HEADS_OWN):
            weighted = (f.decay(k) * f.scores).astype(BF16)
            inner.append(mm(weighted, f.head(f.scaled_n, k)))
        entering = state[...]
        states[c] = entering
        through = mm(f.c, entering.astype(BF16))
        out = jnp.concatenate(inner, axis=1) + through * f.head_in + sm.skip * f.values
        ssd[at, :] = out
        state[...] = f.carry * entering + mm_tn(f.b, f.tail_scaled.astype(BF16))
        mixed = out * f.gate_act
        first = jnp.sum(mixed * mixed, axis=1, keepdims=True)
        second = jnp.sum(d_gated[at, :] * sm.gated_gain * mixed, axis=1, keepdims=True)
        both = jnp.where(lane_iota(CHUNK) == 0, first, second)
        sums_ref[:, at] = both.T[0:8, :]
        return carry

    lax.fori_loop(0, tokens // CHUNK, chunk, 0)


def fold(value):
    rows, width = value.shape
    return jnp.sum(value.reshape(rows // 8, 8, width), axis=0)


def backward_kernel(
    plan, place, sc, row_map, tok, segr, sums_ref, proj, ssd, d_gated, states, w_sf, w_out,
    small_ref, spread, x_hat, cots, *refs
):
    dp = plan.dp
    blocks_out, act_out, back_out = refs[:dp], refs[dp], refs[dp + 1]
    (blocks, xf, dcf, adjoint, gated, dn, colbuf, acc_gg, acc_skip, acc_conv, acc_head, acc_ng,
     wide_out, sem) = refs[dp + 2 :]
    tokens = proj.shape[0]
    piece = tokens // GROUP
    rank, group = sc[0], sc[1]
    chunks = tokens // CHUNK
    sm = Small(small_ref[...], rank)
    fill_xf(xf, proj, tokens)
    for ref in (dcf, adjoint, colbuf, acc_gg, acc_skip, acc_conv, acc_head, acc_ng):
        ref[...] = jnp.zeros_like(ref)
    lane = lane_iota(CHUNK)

    def chunk(i, carry):
        c = chunks - 1 - i
        start = pl.multiple_of(c * CHUNK, CHUNK)
        at = pl.ds(start, CHUNK)
        f = Front(c, rank, sm, xf, proj, tok, segr)
        both = jnp.concatenate([sums_ref[:, at]] * (CHUNK // 8), axis=0).T
        norm = lax.rsqrt(both[:, 0:1] * (1.0 / INNER) + NORM_EPS)
        drag = norm * (both[:, 1:2] * (1.0 / INNER))
        out = ssd[at, :]
        dg = d_gated[at, :]
        unit = out * f.gate_act * norm
        gated[at, :] = (unit * sm.gated_gain).astype(BF16)
        acc_gg[...] += fold(dg * unit)
        d_mixed = norm * (dg * sm.gated_gain - unit * drag)
        d_ssd = d_mixed * f.gate_act
        d_gate = d_mixed * out * (f.gate_sig * (1.0 + f.gate * (1.0 - f.gate_sig)))
        acc_skip[...] += fold(d_ssd * f.values)
        d_ssd_n = d_ssd.astype(BF16)
        entering = states[c]
        entering_n = entering.astype(BF16)
        leaving = adjoint[...]
        leaving_n = leaving.astype(BF16)
        head_ssd = f.head_in * d_ssd
        head_ssd_n = head_ssd.astype(BF16)
        through = mm(f.c, entering_n)
        exit_b = mm(f.b, leaving_n)
        tail_flow = f.tail_scaled * exit_b
        last_row = jnp.sum(tail_flow, axis=0, keepdims=True) + f.carry * jnp.sum(
            leaving * entering, axis=0, keepdims=True
        )
        row = lax.broadcasted_iota(jnp.int32, (CHUNK, OWN), 0)
        flow = head_ssd * through - tail_flow + jnp.where(row == CHUNK - 1, last_row, 0.0)
        d_scores = jnp.zeros((CHUNK, CHUNK), F32)
        d_scaled = []
        row_sums = jnp.zeros((CHUNK, LANES), F32)
        for k in range(HEADS_OWN):
            decay = f.decay(k)
            weighted = decay * f.scores
            d_head = f.head(d_ssd_n, k)
            d_weighted = mm_nt(d_head, f.head(f.scaled_n, k))
            d_scaled.append(mm_tn(weighted.astype(BF16), d_head))
            d_scores = d_scores + d_weighted * decay
            flows = d_weighted * weighted
            row_sums = jnp.where(lane == 4 * k, jnp.sum(flows, axis=1, keepdims=True), row_sums)
            colbuf[4 * k : 4 * k + 1, :] = jnp.sum(flows, axis=0, keepdims=True)
        d_scaled = jnp.concatenate(d_scaled, axis=1) + f.tail * exit_b
        d_scores_n = d_scores.astype(BF16)
        d_c = mm_nt(head_ssd_n, entering_n) + mm(d_scores_n, f.b)
        d_b = mm_tn(d_scores_n, f.c) + mm_nt(f.tail_scaled.astype(BF16), leaving_n)
        adjoint[...] = f.carry * leaving + mm_tn(f.c, head_ssd_n)
        d_sums = row_sums - colbuf[...].T + head_sums(flow)
        upper = triangle(False).astype(BF16)
        high, middle, low = thirds(d_sums)
        d_log = mm(upper, high) + (mm(upper, middle) + mm(upper, low))
        d_values = sm.skip * d_ssd + d_scaled * f.step_wide
        d_step = head_sums(d_scaled * f.values) + d_log * sm.rate
        d_raw = jnp.where(sm.heads, d_step * jax.nn.sigmoid(f.pre), 0.0)
        acc_head[0:8, :] += fold(d_raw)
        acc_head[8:16, :] += fold(d_log * f.step) * sm.rate
        d_act = jnp.concatenate([d_values, d_b, d_c], axis=1)
        d_conv = d_act * (f.conv_sig * (1.0 + f.conv * (1.0 - f.conv_sig)))
        acc_conv[8 * KERNEL : 8 * KERNEL + 8, :] += fold(d_conv)
        acc_conv[8 * (KERNEL - 1) : 8 * KERNEL, :] += fold(d_conv * f.shifted[0])
        for d in range(1, KERNEL):
            lower = 8 * (KERNEL - 1 - d)
            acc_conv[lower : lower + 8, :] += fold(d_conv * f.shifted[d] * f.masks[d])
        dcf[at, :] = d_conv
        window = dcf[pl.ds(start, CHUNK + 8), :]
        masks = tok[pl.ds(start, CHUNK + 8), :]
        d_x = sm.taps[KERNEL - 1] * d_conv
        for d in range(1, KERNEL):
            masked = window * masks[:, d : d + 1]
            d_x = d_x + sm.taps[KERNEL - 1 - d] * masked[d : d + CHUNK]
        dn[at, 0:OWN] = d_gate.astype(BF16)
        dn[at, OWN : OWN + MIXED] = d_x.astype(BF16)
        dn[at, WIDE - LANES :] = pltpu.roll(d_raw, rank, 1).astype(BF16)
        return carry

    lax.fori_loop(0, chunks, chunk, 0)
    chosen = (
        lax.broadcasted_iota(jnp.int32, (D, plan.depth), 0) == row_map[...]
    ).astype(BF16)

    for token_group in range(GROUP):
        rel = token_group ^ rank
        at = slice(token_group * piece, (token_group + 1) * piece)
        act_out[lax.rem(rel, 2), rel // 2] = mm(gated[at, :], w_out[...]).astype(BF16)
        wide = mm_nt(dn[at, :], w_sf[...]).astype(BF16)
        d_normed = mm_nt(wide, chosen)
        back_out[lax.rem(rel, 2), rel // 2] = d_normed.astype(BF16)
        acc_ng[...] += fold(d_normed * x_hat[at, :].astype(F32))

    line = dp // 2

    def slot(i):
        to = i // GROUP
        return lax.rem(to // 2 + line - group // 2, line) * 2 + (lax.rem(to + group, 2))

    span = SLABS if plan.depth <= 2048 else OWN_SLABS
    for first in range(0, SLABS, span):
        grad_in = mm_tn(spread[...], dn[:, first * LANES : (first + span) * LANES])
        for i in range(plan.first_out + 1):
            depth, at = plan.pads[i], plan.offsets[i]
            to = slot(i)
            for j in range(span):
                base = (first + j) * depth
                blocks[to, i % GROUP, base : base + depth, :] = grad_in[
                    at : at + depth, j * LANES : (j + 1) * LANES
                ].astype(BF16)
    grad_out = mm_tn(gated[...], cots[...])
    for j in range(OUT_SLABS):
        wide_out[j, 0:OWN, :] = grad_out[:, j * LANES : (j + 1) * LANES]
        wide_out[j, OWN:, :] = jnp.zeros((plan.frame_rows, LANES), F32)
    for i in range(plan.first_out, plan.count):
        rows, base = (plan.edge_out, plan.edge_at) if i == plan.first_out else (plan.frame_rows, 0)
        at = place[i * GROUP + rank]
        if plan.frame_rows == HEAD_DIM:
            at = pl.multiple_of(at, HEAD_DIM)
        to = slot(i)
        for j in range(OUT_SLABS):
            blocks[to, i % GROUP, base + j * rows : base + (j + 1) * rows, :] = wide_out[
                j, pl.ds(at, rows), :
            ].astype(BF16)
    tail = []
    for k in range(KERNEL + 1):
        line_sum = jnp.sum(acc_conv[8 * k : 8 * k + 8, :], axis=0, keepdims=True)
        tail += [line_sum[:, m * LANES : (m + 1) * LANES] for m in range(5)]
    gain = jnp.sum(acc_ng[...], axis=0, keepdims=True)
    tail += [gain[:, m * LANES : (m + 1) * LANES] for m in range(OUT_SLABS)]
    gain = jnp.sum(acc_gg[...], axis=0, keepdims=True)
    tail += [gain[:, m * LANES : (m + 1) * LANES] for m in range(OWN_SLABS)]
    bias = jnp.sum(acc_head[0:8, :], axis=0, keepdims=True)
    rate = jnp.sum(acc_head[8:16, :], axis=0, keepdims=True)
    skip = jnp.sum(head_sums(acc_skip[...]), axis=0, keepdims=True)
    heads = sm.heads
    vec = pltpu.roll(jnp.where(heads, bias, 0.0), rank, 1)
    vec = vec + pltpu.roll(jnp.where(heads, rate, 0.0), rank + HEADS, 1)
    vec = vec + pltpu.roll(jnp.where(heads, skip, 0.0), rank + 2 * HEADS, 1)
    tail += [vec, jnp.zeros((SMALL - len(tail) - 1, LANES), F32)]
    blocks[slot(plan.count - 1), GROUP - 1, plan.frame : plan.frame + SMALL, :] = jnp.concatenate(
        tail, axis=0
    ).astype(BF16)
    copies = [
        pltpu.make_async_copy(blocks.at[j], blocks_out[j], sem.at[j]) for j in range(dp)
    ]
    for copy in copies:
        copy.start()
    for copy in copies:
        copy.wait()


def any_spec():
    return pl.BlockSpec(memory_space=pl.ANY)


def vmem_spec():
    return pl.BlockSpec(memory_space=pltpu.VMEM)


def smem_spec():
    return pl.BlockSpec(memory_space=pltpu.SMEM)


def params_of(flops, moved, limit=38 * MIB):
    return {
        "compiler_params": pltpu.CompilerParams(vmem_limit_bytes=limit),
        "cost_estimate": pl.CostEstimate(
            flops=int(flops), bytes_accessed=int(moved), transcendentals=0
        ),
    }


def shape(dims, dtype):
    return jax.ShapeDtypeStruct(dims, dtype)


def swap(value, axis, flip):
    count = lax.axis_size(axis)
    return lax.ppermute(value, axis, [(i, i ^ flip) for i in range(count)])


def along(value):
    count = lax.axis_size("dp")
    return lax.ppermute(value, "dp", [(i, (i + 2) % count) for i in range(count)])


def pieces_of(value):
    across = swap(value, "seq", 2)
    close = swap(value, "seq", 1)
    return [value, close, across, swap(across, "seq", 1)]


def sum_pieces(value):
    got = swap(value[1], "seq", 1)
    half = (value[0].astype(F32) + got.astype(F32)).astype(BF16)
    other = swap(half[1], "seq", 2)
    return half[0].astype(F32) + other.astype(F32)


def local(inputs, out_grad, segment_ids, params, moment_one, moment_two):
    dp, seq = lax.axis_size("dp"), lax.axis_size("seq")
    length = params.shape[0]
    plan = Plan(dp, seq, length)
    piece = inputs.shape[1]
    tokens = piece * seq
    group, rank = lax.axis_index("dp"), lax.axis_index("seq")
    line = dp // 2
    sublanes = length // LANES
    scratch_rows = up(PAD + sublanes + PAD, 8)
    block = plan.block
    where = plan.scalars(group * seq + rank)
    sc = jnp.stack([rank, group]).astype(jnp.int32)
    place = jnp.asarray(plan.place.reshape(-1))
    row_map = jnp.asarray(plan.row_map)

    flat_params = params.reshape(sublanes, LANES)
    packed = pl.pallas_call(
        functools.partial(pack_kernel, plan),
        out_shape=shape((GROUP, block, LANES), BF16),
        in_specs=[smem_spec(), vmem_spec()],
        out_specs=vmem_spec(),
        scratch_shapes=[
            pltpu.VMEM((scratch_rows, LANES), F32),
            pltpu.VMEM((plan.pure * ROW_SLABS, LANES), F32),
            pltpu.VMEM((plan.frame, LANES), F32),
            pltpu.VMEM((SMALL, LANES), F32),
        ],
        name="pack",
        **params_of(1e6, 2e6),
    )(where, flat_params)
    x_pieces = pieces_of(inputs[0])
    cot = out_grad[0].astype(BF16)
    c_pieces = pieces_of(cot)
    mine = lax.all_to_all(packed, "seq", 0, 0)
    weights = [mine, swap(mine, "dp", 1)]
    ring = mine
    for _ in range(1, line):
        ring = along(ring)
        weights += [ring, swap(ring, "dp", 1)]

    ids = segment_ids[0]
    chunks = tokens // CHUNK
    spot = jnp.arange(tokens)
    by_chunk = ids.reshape(chunks, CHUNK)
    last = by_chunk[:, CHUNK - 1]
    prior = jnp.concatenate([jnp.full((1,), -1, jnp.int32), last[:-1]])
    columns = [ids.astype(F32)]
    for d in range(1, KERNEL):
        earlier = jnp.concatenate([jnp.full((d,), -1, jnp.int32), ids[:-d]])
        columns.append((earlier == ids).astype(F32))
    columns.append((by_chunk == prior[:, None]).reshape(-1).astype(F32))
    columns.append((by_chunk == last[:, None]).reshape(-1).astype(F32))
    columns.append(
        jnp.broadcast_to((last == prior)[:, None], by_chunk.shape).reshape(-1).astype(F32)
    )
    tok = jnp.pad(jnp.stack(columns, axis=1), ((0, 8), (0, LANES - len(columns))))
    segr = by_chunk.astype(F32)

    depth = plan.depth
    limit = 38 * MIB if depth <= 2048 else 63 * MIB
    forward = pl.pallas_call(
        functools.partial(forward_kernel, plan),
        out_shape=[
            shape((tokens, WIDE), BF16),
            shape((tokens, OWN), F32),
            shape((tokens, OWN), F32),
            shape((chunks, STATE, OWN), F32),
            shape((8, tokens), F32),
            shape((depth, WIDE), BF16),
            shape((OWN, D), BF16),
            shape((SMALL, LANES), F32),
            shape((tokens, depth), BF16),
            shape((tokens, D), BF16),
            shape((tokens, D), BF16),
        ],
        in_specs=[smem_spec(), smem_spec(), vmem_spec(), vmem_spec(), vmem_spec()]
        + [any_spec()] * (2 * GROUP + dp),
        out_specs=[vmem_spec()] * 11,
        scratch_shapes=[
            pltpu.VMEM((tokens, D), F32),
            pltpu.VMEM((dp, GROUP, block, LANES), BF16),
            pltpu.VMEM((OUT_SLABS, OWN + plan.frame_rows, LANES), F32),
            pltpu.VMEM((tokens + 8, MIXED), F32),
            pltpu.VMEM((STATE, OWN), F32),
            pltpu.SemaphoreType.DMA((dp + 2 * GROUP,)),
        ],
        name="forward",
        **params_of(8e9, 3e7, limit),
    )(place, sc, row_map, tok, segr, *x_pieces, *c_pieces, *weights)
    proj, ssd, d_gated, states, sums, w_sf, w_out, small, spread, x_hat, cots = forward
    sums = sums + swap(sums, "seq", 1)
    sums = sums + swap(sums, "seq", 2)

    backward = pl.pallas_call(
        functools.partial(backward_kernel, plan),
        out_shape=[shape((GROUP, block, LANES), BF16)] * dp
        + [shape((2, 2, piece, D), BF16)] * 2,
        in_specs=[smem_spec(), smem_spec()] + [vmem_spec()] * 14,
        out_specs=[any_spec()] * dp + [vmem_spec()] * 2,
        scratch_shapes=[
            pltpu.VMEM((dp, GROUP, block, LANES), BF16),
            pltpu.VMEM((tokens + 8, MIXED), F32),
            pltpu.VMEM((tokens + 8, MIXED), F32),
            pltpu.VMEM((STATE, OWN), F32),
            pltpu.VMEM((tokens, OWN), BF16),
            pltpu.VMEM((tokens, WIDE), BF16),
            pltpu.VMEM((CHUNK, LANES), F32),
            pltpu.VMEM((8, OWN), F32),
            pltpu.VMEM((8, OWN), F32),
            pltpu.VMEM((8 * (KERNEL + 1), MIXED), F32),
            pltpu.VMEM((16, LANES), F32),
            pltpu.VMEM((8, D), F32),
            pltpu.VMEM((OUT_SLABS, OWN + plan.frame_rows, LANES), F32),
            pltpu.SemaphoreType.DMA((dp,)),
        ],
        name="backward",
        **params_of(16e9, 4e7, limit),
    )(place, sc, row_map, tok, segr, sums, proj, ssd, d_gated, states, w_sf, w_out, small, spread,
      x_hat, cots)
    terms, act_terms, back_terms = backward[:dp], backward[dp], backward[dp + 1]

    def joined(a, b):
        return (a.astype(F32) + b.astype(F32)).astype(BF16)

    def column(j):
        return joined(terms[2 * j], swap(terms[2 * j + 1], "dp", 1))

    moving = None
    for j in range(line - 1, 0, -1):
        here = column(j)
        moving = along(here if moving is None else joined(here, moving))
    here = column(0)
    reduced = here if moving is None else joined(here, moving)
    blocks = lax.all_to_all(reduced, "seq", 0, 0)

    flat_shape = shape((sublanes, LANES), F32)
    updated = pl.pallas_call(
        functools.partial(unpack_kernel, plan),
        out_shape=[flat_shape] * 4,
        in_specs=[smem_spec()] + [vmem_spec()] * 4,
        out_specs=[vmem_spec()] * 4,
        scratch_shapes=[
            pltpu.VMEM((scratch_rows, LANES), F32),
            pltpu.VMEM((plan.pure * ROW_SLABS, LANES), F32),
            pltpu.VMEM((plan.frame, LANES), F32),
        ],
        name="unpack",
        **params_of(1e6, 5e6),
    )(
        where,
        blocks,
        flat_params,
        moment_one.reshape(sublanes, LANES),
        moment_two.reshape(sublanes, LANES),
    )
    grad, new_params, new_one, new_two = [value.reshape(length) for value in updated]

    residual = inputs[0]
    activation = residual + sum_pieces(act_terms)
    d_normed = sum_pieces(back_terms)
    inv_rms = lax.rsqrt(jnp.mean(residual * residual, axis=-1, keepdims=True) + NORM_EPS)
    hat = residual * inv_rms
    norm_gain = small[25:31].reshape(D)
    d_hat = d_normed * norm_gain
    d_front = inv_rms * (d_hat - hat * jnp.mean(d_hat * hat, axis=-1, keepdims=True))
    gradient = out_grad[0] + d_front
    return (activation[None], gradient[None], grad, new_params, new_one, new_two)


def solution(mesh):
    tokens = P("dp", "seq", None)
    flat = P(("dp", "seq"))

    return jax.shard_map(
        local,
        mesh=mesh,
        in_specs=(tokens, tokens, P("dp", None), flat, flat, flat),
        out_specs=(tokens, tokens, flat, flat, flat, flat),
        check_vma=False,
    )
```

profile of v0, /device:TPU:0, one launch (start us, length us, event | category | flops | bytes accessed | tf_op | source)
XLA Modules:
  0.0 220.5 jit_solution(405340674330133814)
XLA Ops:
  2.1 5.1 %pack.1 = bf16[4,432,128]{2,1,0:T(8,128)(2,1)} custom-call(s32[12]{0:T(128)S(1)} %stack.92.sc, f32[920,128]{1,0:T(8,128)S(1)} %bitcast.85), custom_call_target="tpu_custom_call" | custom-call | flops 1000000 | bytes 2000000 | tf_op jit(solution)/shard_map/pack/pallas_call | solution.py:806
  7.2 4.2 %all-to-all-start = ((bf16[4,432,128]{2,1,0:T(8,128)(2,1)}), bf16[4,432,128]{2,1,0:T(8,128)(2,1)S(1)}, u32[]{:S(2)}, u32[]{:S(2)}) async-start(bf16[4,432,128]{2,1,0:T(8,128)(2,1)} %pack.1), calls=%async_computation | async-start | bytes 884736 | tf_op jit(solution)/shard_map/all_to_all | solution.py:823
  11.5 2.3 %collective-permute-start.1 = (f32[256,768]{1,0:T(8,128)S(1)}, f32[256,768]{1,0:T(8,128)S(1)}, u32[]{:S(2)}, u32[]{:S(2)}) collective-permute-start(f32[256,768]{1,0:T(8,128)S(1)} %bitcast.82), channel_id=1, source_target_pairs={{0,2},{1,3},{2,0},{3,1},{4,6},{5,7},{6,4},{7,5},{8,10},{9,11},{10,... | collective-permute-start | bytes 2359304 | tf_op jit(solution)/shard_map/ppermute | solution.py:768
  13.7 6.4 %all-to-all-done.refs_8_ = bf16[4,432,128]{2,1,0:T(8,128)(2,1)S(1)} async-done(((bf16[4,432,128]{2,1,0:T(8,128)(2,1)}), bf16[4,432,128]{2,1,0:T(8,128)(2,1)S(1)}, u32[]{:S(2)}, u32[]{:S(2)}) %all-to-all-start) | async-done | bytes 442400 | tf_op jit(solution)/shard_map/all_to_all | solution.py:823
  22.4 10.3 %collective-permute-done.7.refs_10_ = bf16[4,432,128]{2,1,0:T(8,128)(2,1)} collective-permute-done((bf16[4,432,128]{2,1,0:T(8,128)(2,1)S(1)}, bf16[4,432,128]{2,1,0:T(8,128)(2,1)}, u32[]{:S(2)}, u32[]{:S(2)}) %collective-permute-start.7) | collective-permute-done | bytes 442400 | tf_op jit(solution)/shard_map/ppermute | solution.py:773
  35.3 9.3 %collective-permute-done.4.refs_6_ = bf16[256,768]{1,0:T(8,128)(2,1)S(1)} collective-permute-done((bf16[256,768]{1,0:T(8,128)(2,1)S(1)}, bf16[256,768]{1,0:T(8,128)(2,1)S(1)}, u32[]{:S(2)}, u32[]{:S(2)}) %collective-permute-start.4) | collective-permute-done | bytes 393248 | tf_op jit(solution)/shard_map/ppermute | solution.py:768
  45.4 2.3 %collective-permute-start.11 = (bf16[4,432,128]{2,1,0:T(8,128)(2,1)}, bf16[4,432,128]{2,1,0:T(8,128)(2,1)}, u32[]{:S(2)}, u32[]{:S(2)}) collective-permute-start(bf16[4,432,128]{2,1,0:T(8,128)(2,1)} %collective-permute-done.9.refs_12_), channel_id=1, source_target_pairs={{0,8},{4,12},{8,16},{12,20},{16,24},{20,28},{24,0},{28,4},{1,9},{5... | collective-permute-start | bytes 1327112 | tf_op jit(solution)/shard_map/ppermute | solution.py:773
  52.9 7.2 %collective-permute-done.11.refs_14_ = bf16[4,432,128]{2,1,0:T(8,128)(2,1)} collective-permute-done((bf16[4,432,128]{2,1,0:T(8,128)(2,1)}, bf16[4,432,128]{2,1,0:T(8,128)(2,1)}, u32[]{:S(2)}, u32[]{:S(2)}) %collective-permute-start.11) | collective-permute-done | bytes 442400 | tf_op jit(solution)/shard_map/ppermute | solution.py:773
  60.1 2.2 collective-permute-start.12
  64.9 8.1 %collective-permute-done.10.refs_13_ = bf16[4,432,128]{2,1,0:T(8,128)(2,1)} collective-permute-done((bf16[4,432,128]{2,1,0:T(8,128)(2,1)}, bf16[4,432,128]{2,1,0:T(8,128)(2,1)}, u32[]{:S(2)}, u32[]{:S(2)}) %collective-permute-start.10) | collective-permute-done | bytes 442400 | tf_op jit(solution)/shard_map/ppermute | solution.py:768
  73.0 8.7 %collective-permute-done.12.refs_15_ = bf16[4,432,128]{2,1,0:T(8,128)(2,1)} collective-permute-done((bf16[4,432,128]{2,1,0:T(8,128)(2,1)}, bf16[4,432,128]{2,1,0:T(8,128)(2,1)}, u32[]{:S(2)}, u32[]{:S(2)}) %collective-permute-start.12) | collective-permute-done | bytes 442400 | tf_op jit(solution)/shard_map/ppermute | solution.py:768
  85.7 27.9 %forward.1 = (bf16[1024,1152]{1,0:T(8,128)(2,1)}, f32[1024,384]{1,0:T(8,128)S(1)}, f32[1024,384]{1,0:T(8,128)S(1)}, f32[8,128,384]{2,1,0:T(8,128)S(1)}, f32[8,10...) custom-call(s32[128]{0:T(128)S(1)} %copy-done.14, ...), custom_call_target="tpu_custom_call" | custom-call | flops 8000000000 | bytes 30000000 | tf_op jit(solution)/shard_map/forward/pallas_call | solution.py:850
  115.5 3.4 %collective-permute-done.14 = f32[8,1024]{1,0:T(8,128)S(1)} collective-permute-done((f32[8,1024]{1,0:T(8,128)S(1)}, f32[8,1024]{1,0:T(8,128)S(1)}, u32[]{:S(2)}, u32[]{:S(2)}) %collective-permute-start.14) | collective-permute-done | bytes 32800 | tf_op jit(solution)/shard_map/ppermute | solution.py:768
  120.3 37.2 %backward.1 = (bf16[4,432,128]{2,1,0:T(8,128)(2,1)S(1)}, bf16[4,432,128]{2,1,0:T(8,128)(2,1)S(1)}, bf16[4,432,128]{2,1,0:T(8,128)(2,1)S(1)}, bf16[4,432,128]{2,1...) custom-call(s32[128]{0:T(128)S(1)} %copy-done.14, ...), custom_call_target="tpu_custom_call" | custom-call | flops 16000000000 | bytes 40000000 | tf_op jit(solution)/shard_map/backward/pallas_call | solution.py:883
  161.8 8.8 %collective-permute-done.22 = bf16[4,432,128]{2,1,0:T(8,128)(2,1)S(1)} collective-permute-done((bf16[4,432,128]{2,1,0:T(8,128)(2,1)S(1)}, bf16[4,432,128]{2,1,0:T(8,128)(2,1)S(1)}, u32[]{:S(2)}, u32[]{:S(2)}) %collective-permute-start.22) | collective-permute-done | bytes 442400 | tf_op jit(solution)/shard_map/ppermute | solution.py:768
  172.6 7.4 %collective-permute-done.21 = bf16[4,432,128]{2,1,0:T(8,128)(2,1)S(1)} collective-permute-done((bf16[4,432,128]{2,1,0:T(8,128)(2,1)S(1)}, bf16[4,432,128]{2,1,0:T(8,128)(2,1)S(1)}, u32[]{:S(2)}, u32[]{:S(2)}) %collective-permute-start.21) | collective-permute-done | bytes 442400 | tf_op jit(solution)/shard_map/ppermute | solution.py:768
  182.5 7.0 %collective-permute-done.20 = bf16[4,432,128]{2,1,0:T(8,128)(2,1)S(1)} collective-permute-done((bf16[4,432,128]{2,1,0:T(8,128)(2,1)S(1)}, bf16[4,432,128]{2,1,0:T(8,128)(2,1)S(1)}, u32[]{:S(2)}, u32[]{:S(2)}) %collective-permute-start.20) | collective-permute-done | bytes 442400 | tf_op jit(solution)/shard_map/ppermute | solution.py:768
  189.5 2.5 %collective-permute-done.24 = bf16[4,432,128]{2,1,0:T(8,128)(2,1)S(1)} collective-permute-done((bf16[4,432,128]{2,1,0:T(8,128)(2,1)S(1)}, bf16[4,432,128]{2,1,0:T(8,128)(2,1)S(1)}, u32[]{:S(2)}, u32[]{:S(2)}) %collective-permute-start.24) | collective-permute-done | bytes 442400 | tf_op jit(solution)/shard_map/ppermute | solution.py:773
  193.7 3.3 %collective-permute-done.19 = bf16[4,432,128]{2,1,0:T(8,128)(2,1)S(1)} collective-permute-done((bf16[4,432,128]{2,1,0:T(8,128)(2,1)S(1)}, bf16[4,432,128]{2,1,0:T(8,128)(2,1)S(1)}, u32[]{:S(2)}, u32[]{:S(2)}) %collective-permute-start.19) | collective-permute-done | bytes 442400 | tf_op jit(solution)/shard_map/ppermute | solution.py:768
  197.0 5.3 %collective-permute-done.25 = bf16[4,432,128]{2,1,0:T(8,128)(2,1)S(1)} collective-permute-done((bf16[4,432,128]{2,1,0:T(8,128)(2,1)S(1)}, bf16[4,432,128]{2,1,0:T(8,128)(2,1)S(1)}, u32[]{:S(2)}, u32[]{:S(2)}) %collective-permute-start.25) | collective-permute-done | bytes 442400 | tf_op jit(solution)/shard_map/ppermute | solution.py:773
  203.3 3.5 %all-to-all-start.1 = ((bf16[4,432,128]{2,1,0:T(8,128)(2,1)}), bf16[4,432,128]{2,1,0:T(8,128)(2,1)S(1)}, u32[]{:S(2)}, u32[]{:S(2)}) async-start(bf16[4,432,128]{2,1,0:T(8,128)(2,1)} %add_convert_fusion), calls=%async_computation.1 | async-start | bytes 884736 | tf_op jit(solution)/shard_map/all_to_all | solution.py:923
  206.8 3.1 %fusion.5 = (f32[1,256,768]{2,1,0:T(8,128)}, f32[1,256,768]{2,1,0:T(8,128)}) fusion(f32[1,256,768]{2,1,0:T(8,128)} %param.9, bf16[256,768]{1,0:T(8,128)(2,1)} %copy-done.18, f32[256]{0:T(256)S(1)} %broadcast_multiply_fusion, f32[768]{0:T(1024)S(1)} %slice_bitcast_fusion.6, f32[256]{0:T(256)S(1)} %add_rsqrt_fusion, bf16[2,256,768]{2,1,0:T(8,128)(2,1)S(1)} %fusion, ...), kind=kLoop, calls=%fused_computation.18 | loop fusion | flops 2555904 | bytes 4723712 | tf_op jit(solution)/shard_map/broadcast_in_dim | solution.py:956
  209.8 4.8 %all-to-all-done.1.blk = bf16[4,432,128]{2,1,0:T(8,128)(2,1)S(1)} async-done(((bf16[4,432,128]{2,1,0:T(8,128)(2,1)}), bf16[4,432,128]{2,1,0:T(8,128)(2,1)S(1)}, u32[]{:S(2)}, u32[]{:S(2)}) %all-to-all-start.1) | async-done | bytes 442400 | tf_op jit(solution)/shard_map/all_to_all | solution.py:923
  214.6 5.8 %unpack.1 = (f32[920,128]{1,0:T(8,128)}, f32[920,128]{1,0:T(8,128)}, f32[920,128]{1,0:T(8,128)}, f32[920,128]{1,0:T(8,128)}) custom-call(s32[12]{0:T(128)S(1)} %stack.92.sc, bf16[4,432,128]{2,1,0:T(8,128)(2,1)S(1)} %all-to-all-done.1.blk, f32[920,128]{1,0:T(8,128)S(1)} %bitcast.86, f32[920,128]{1,0:T(8,128)S(1)} %bitcast.87, f32[920,128]{1,0:T(8,128)S(1)} %bitcast.88), custom_call_target="tpu_custom_call" | custom-call | flops 1000000 | bytes 5000000 | tf_op jit(solution)/shard_map/unpack/pallas_call | solution.py:926
  (112 shorter events, 33.4 us)
Async XLA Ops:
  7.2 12.9 %all-to-all-start = ((bf16[4,432,128]{2,1,0:T(8,128)(2,1)}), bf16[4,432,128]{2,1,0:T(8,128)(2,1)S(1)}, u32[]{:S(2)}, u32[]{:S(2)}) async-start(bf16[4,432,128]{2,1,0:T(8,128)(2,1)} %pack.1), calls=%async_computation | async-start | bytes 884736 | tf_op jit(solution)/shard_map/all_to_all | solution.py:823
  11.5 37.4 %collective-permute-start.1 = (f32[256,768]{1,0:T(8,128)S(1)}, f32[256,768]{1,0:T(8,128)S(1)}, u32[]{:S(2)}, u32[]{:S(2)}) collective-permute-start(f32[256,768]{1,0:T(8,128)S(1)} %bitcast.82), channel_id=1, source_target_pairs={{0,2},{1,3},{2,0},{3,1},{4,6},{5,7},{6,4},{7,5},{8,10},{9,11},{10,... | collective-permute-start | bytes 2359304 | tf_op jit(solution)/shard_map/ppermute | solution.py:768
  20.1 12.6 %collective-permute-start.7 = (bf16[4,432,128]{2,1,0:T(8,128)(2,1)S(1)}, bf16[4,432,128]{2,1,0:T(8,128)(2,1)}, u32[]{:S(2)}, u32[]{:S(2)}) collective-permute-start(bf16[4,432,128]{2,1,0:T(8,128)(2,1)S(1)} %all-to-all-done.refs_8_), channel_id=1, source_target_pairs={{0,8},{4,12},{8,16},{12,20},{16,24},{20,28},{24,0},{28,4},{1,9},{5... | collective-permute-start | bytes 1327112 | tf_op jit(solution)/shard_map/ppermute | solution.py:773
  22.3 22.4 %collective-permute-start.4 = (bf16[256,768]{1,0:T(8,128)(2,1)S(1)}, bf16[256,768]{1,0:T(8,128)(2,1)S(1)}, u32[]{:S(2)}, u32[]{:S(2)}) collective-permute-start(bf16[256,768]{1,0:T(8,128)(2,1)S(1)} %bitcast_convert_fusion.refs_4_), channel_id=1, source_target_pairs={{0,2},{1,3},{2,0},{3,1},{4,6},{5,7},{6,4},{7,5},{8,10},{9,11},{10,... | collective-permute-start | bytes 1179656 | tf_op jit(solution)/shard_map/ppermute | solution.py:768
  22.3 25.5 %collective-permute-start.3 = (bf16[256,768]{1,0:T(8,128)(2,1)S(1)}, bf16[256,768]{1,0:T(8,128)(2,1)S(1)}, u32[]{:S(2)}, u32[]{:S(2)}) collective-permute-start(bf16[256,768]{1,0:T(8,128)(2,1)S(1)} %bitcast_convert_fusion.refs_4_), channel_id=1, source_target_pairs={{0,1},{1,0},{2,3},{3,2},{4,5},{5,4},{6,7},{7,6},{8,9},{9,8},{10,11... | collective-permute-start | bytes 1179656 | tf_op jit(solution)/shard_map/ppermute | solution.py:768
  32.7 12.7 %collective-permute-start.9 = (bf16[4,432,128]{2,1,0:T(8,128)(2,1)}, bf16[4,432,128]{2,1,0:T(8,128)(2,1)}, u32[]{:S(2)}, u32[]{:S(2)}) collective-permute-start(bf16[4,432,128]{2,1,0:T(8,128)(2,1)} %collective-permute-done.7.refs_10_), channel_id=1, source_target_pairs={{0,8},{4,12},{8,16},{12,20},{16,24},{20,28},{24,0},{28,4},{1,9},{5... | collective-permute-start | bytes 1327112 | tf_op jit(solution)/shard_map/ppermute | solution.py:773
  33.5 15.8 %collective-permute-start.6 = (bf16[4,432,128]{2,1,0:T(8,128)(2,1)S(1)}, bf16[4,432,128]{2,1,0:T(8,128)(2,1)S(1)}, u32[]{:S(2)}, u32[]{:S(2)}) collective-permute-start(bf16[4,432,128]{2,1,0:T(8,128)(2,1)S(1)} %all-to-all-done.refs_8_), channel_id=1, source_target_pairs={{0,4},{4,0},{8,12},{12,8},{16,20},{20,16},{24,28},{28,24},{1,5},{5... | collective-permute-start | bytes 1327112 | tf_op jit(solution)/shard_map/ppermute | solution.py:768
  45.4 14.7 %collective-permute-start.11 = (bf16[4,432,128]{2,1,0:T(8,128)(2,1)}, bf16[4,432,128]{2,1,0:T(8,128)(2,1)}, u32[]{:S(2)}, u32[]{:S(2)}) collective-permute-start(bf16[4,432,128]{2,1,0:T(8,128)(2,1)} %collective-permute-done.9.refs_12_), channel_id=1, source_target_pairs={{0,8},{4,12},{8,16},{12,20},{16,24},{20,28},{24,0},{28,4},{1,9},{5... | collective-permute-start | bytes 1327112 | tf_op jit(solution)/shard_map/ppermute | solution.py:773
  48.6 16.3 %collective-permute-start = (f32[256,768]{1,0:T(8,128)S(1)}, f32[256,768]{1,0:T(8,128)S(1)}, u32[]{:S(2)}, u32[]{:S(2)}) collective-permute-start(f32[256,768]{1,0:T(8,128)S(1)} %bitcast.83), channel_id=1, source_target_pairs={{0,1},{1,0},{2,3},{3,2},{4,5},{5,4},{6,7},{7,6},{8,9},{9,8},{10,11... | collective-permute-start | bytes 2359304 | tf_op jit(solution)/shard_map/ppermute | solution.py:768
  48.8 16.1 %collective-permute-start.2 = (f32[256,768]{1,0:T(8,128)S(1)}, f32[256,768]{1,0:T(8,128)}, u32[]{:S(2)}, u32[]{:S(2)}) collective-permute-start(f32[256,768]{1,0:T(8,128)S(1)} %collective-permute-done.1.refs_2_), channel_id=1, source_target_pairs={{0,1},{1,0},{2,3},{3,2},{4,5},{5,4},{6,7},{7,6},{8,9},{9,8},{10,11... | collective-permute-start | bytes 2359304 | tf_op jit(solution)/shard_map/ppermute | solution.py:768
  50.2 14.8 %collective-permute-start.8 = (bf16[4,432,128]{2,1,0:T(8,128)(2,1)}, bf16[4,432,128]{2,1,0:T(8,128)(2,1)}, u32[]{:S(2)}, u32[]{:S(2)}) collective-permute-start(bf16[4,432,128]{2,1,0:T(8,128)(2,1)} %collective-permute-done.7.refs_10_), channel_id=1, source_target_pairs={{0,4},{4,0},{8,12},{12,8},{16,20},{20,16},{24,28},{28,24},{1,5},{5... | collective-permute-start | bytes 1327112 | tf_op jit(solution)/shard_map/ppermute | solution.py:768
  52.4 20.6 %collective-permute-start.10 = (bf16[4,432,128]{2,1,0:T(8,128)(2,1)}, bf16[4,432,128]{2,1,0:T(8,128)(2,1)}, u32[]{:S(2)}, u32[]{:S(2)}) collective-permute-start(bf16[4,432,128]{2,1,0:T(8,128)(2,1)} %collective-permute-done.9.refs_12_), channel_id=1, source_target_pairs={{0,4},{4,0},{8,12},{12,8},{16,20},{20,16},{24,28},{28,24},{1,5},{5... | collective-permute-start | bytes 1327112 | tf_op jit(solution)/shard_map/ppermute | solution.py:768
  60.1 21.6 %collective-permute-start.12 = (bf16[4,432,128]{2,1,0:T(8,128)(2,1)}, bf16[4,432,128]{2,1,0:T(8,128)(2,1)}, u32[]{:S(2)}, u32[]{:S(2)}) collective-permute-start(bf16[4,432,128]{2,1,0:T(8,128)(2,1)} %collective-permute-done.11.refs_14_), channel_id=1, source_target_pairs={{0,4},{4,0},{8,12},{12,8},{16,20},{20,16},{24,28},{28,24},{1,5},{5... | collective-permute-start | bytes 1327112 | tf_op jit(solution)/shard_map/ppermute | solution.py:768
  157.4 13.1 %collective-permute-start.22 = (bf16[4,432,128]{2,1,0:T(8,128)(2,1)S(1)}, bf16[4,432,128]{2,1,0:T(8,128)(2,1)S(1)}, u32[]{:S(2)}, u32[]{:S(2)}) collective-permute-start(bf16[4,432,128]{2,1,0:T(8,128)(2,1)S(1)} %get-tuple-element.51), channel_id=1, source_target_pairs={{0,4},{4,0},{8,12},{12,8},{16,20},{20,16},{24,28},{28,24},{1,5},{5... | collective-permute-start | bytes 1327112 | tf_op jit(solution)/shard_map/ppermute | solution.py:768
  159.1 13.3 %collective-permute-start.17 = (bf16[2,256,768]{2,1,0:T(8,128)(2,1)S(1)}, bf16[2,256,768]{2,1,0:T(8,128)(2,1)S(1)}, u32[]{:S(2)}, u32[]{:S(2)}) collective-permute-start(bf16[2,256,768]{2,1,0:T(8,128)(2,1)S(1)} %slice_bitcast_fusion), channel_id=1, source_target_pairs={{0,1},{1,0},{2,3},{3,2},{4,5},{5,4},{6,7},{7,6},{8,9},{9,8},{10,11... | collective-permute-start | bytes 2359304 | tf_op jit(solution)/shard_map/ppermute | solution.py:768
  159.2 20.8 %collective-permute-start.21 = (bf16[4,432,128]{2,1,0:T(8,128)(2,1)S(1)}, bf16[4,432,128]{2,1,0:T(8,128)(2,1)S(1)}, u32[]{:S(2)}, u32[]{:S(2)}) collective-permute-start(bf16[4,432,128]{2,1,0:T(8,128)(2,1)S(1)} %get-tuple-element.49), channel_id=1, source_target_pairs={{0,4},{4,0},{8,12},{12,8},{16,20},{20,16},{24,28},{28,24},{1,5},{5... | collective-permute-start | bytes 1327112 | tf_op jit(solution)/shard_map/ppermute | solution.py:768
  159.8 29.8 %collective-permute-start.20 = (bf16[4,432,128]{2,1,0:T(8,128)(2,1)S(1)}, bf16[4,432,128]{2,1,0:T(8,128)(2,1)S(1)}, u32[]{:S(2)}, u32[]{:S(2)}) collective-permute-start(bf16[4,432,128]{2,1,0:T(8,128)(2,1)S(1)} %get-tuple-element.47), channel_id=1, source_target_pairs={{0,4},{4,0},{8,12},{12,8},{16,20},{20,16},{24,28},{28,24},{1,5},{5... | collective-permute-start | bytes 1327112 | tf_op jit(solution)/shard_map/ppermute | solution.py:768
  161.3 35.7 %collective-permute-start.19 = (bf16[4,432,128]{2,1,0:T(8,128)(2,1)S(1)}, bf16[4,432,128]{2,1,0:T(8,128)(2,1)S(1)}, u32[]{:S(2)}, u32[]{:S(2)}) collective-permute-start(bf16[4,432,128]{2,1,0:T(8,128)(2,1)S(1)} %get-tuple-element.45), channel_id=1, source_target_pairs={{0,4},{4,0},{8,12},{12,8},{16,20},{20,16},{24,28},{28,24},{1,5},{5... | collective-permute-start | bytes 1327112 | tf_op jit(solution)/shard_map/ppermute | solution.py:768
  170.7 10.2 %collective-permute-start.23 = (bf16[4,432,128]{2,1,0:T(8,128)(2,1)S(1)}, bf16[4,432,128]{2,1,0:T(8,128)(2,1)S(1)}, u32[]{:S(2)}, u32[]{:S(2)}) collective-permute-start(bf16[4,432,128]{2,1,0:T(8,128)(2,1)S(1)} %add_convert_fusion.3), channel_id=1, source_target_pairs={{0,8},{4,12},{8,16},{12,20},{16,24},{20,28},{24,0},{28,4},{1,9},{5... | collective-permute-start | bytes 1327112 | tf_op jit(solution)/shard_map/ppermute | solution.py:773
  181.0 11.0 %collective-permute-start.24 = (bf16[4,432,128]{2,1,0:T(8,128)(2,1)S(1)}, bf16[4,432,128]{2,1,0:T(8,128)(2,1)S(1)}, u32[]{:S(2)}, u32[]{:S(2)}) collective-permute-start(bf16[4,432,128]{2,1,0:T(8,128)(2,1)S(1)} %add_convert_fusion.2), channel_id=1, source_target_pairs={{0,8},{4,12},{8,16},{12,20},{16,24},{20,28},{24,0},{28,4},{1,9},{5... | collective-permute-start | bytes 1327112 | tf_op jit(solution)/shard_map/ppermute | solution.py:773
  181.9 11.5 %collective-permute-start.18 = (bf16[256,768]{1,0:T(8,128)(2,1)S(1)}, bf16[256,768]{1,0:T(8,128)(2,1)S(1)}, u32[]{:S(2)}, u32[]{:S(2)}) collective-permute-start(bf16[256,768]{1,0:T(8,128)(2,1)S(1)} %slice_bitcast_fusion.2), channel_id=1, source_target_pairs={{0,2},{1,3},{2,0},{3,1},{4,6},{5,7},{6,4},{7,5},{8,10},{9,11},{10,... | collective-permute-start | bytes 1179656 | tf_op jit(solution)/shard_map/ppermute | solution.py:768
  192.2 10.2 %collective-permute-start.25 = (bf16[4,432,128]{2,1,0:T(8,128)(2,1)S(1)}, bf16[4,432,128]{2,1,0:T(8,128)(2,1)S(1)}, u32[]{:S(2)}, u32[]{:S(2)}) collective-permute-start(bf16[4,432,128]{2,1,0:T(8,128)(2,1)S(1)} %add_convert_fusion.1), channel_id=1, source_target_pairs={{0,8},{4,12},{8,16},{12,20},{16,24},{20,28},{24,0},{28,4},{1,9},{5... | collective-permute-start | bytes 1327112 | tf_op jit(solution)/shard_map/ppermute | solution.py:773
  193.0 13.8 %collective-permute-start.16 = (bf16[256,768]{1,0:T(8,128)(2,1)}, bf16[256,768]{1,0:T(8,128)(2,1)}, u32[]{:S(2)}, u32[]{:S(2)}) collective-permute-start(bf16[256,768]{1,0:T(8,128)(2,1)} %slice_bitcast_fusion.4), channel_id=1, source_target_pairs={{0,2},{1,3},{2,0},{3,1},{4,6},{5,7},{6,4},{7,5},{8,10},{9,11},{10,... | collective-permute-start | bytes 1179656 | tf_op jit(solution)/shard_map/ppermute | solution.py:768
  203.3 11.4 %all-to-all-start.1 = ((bf16[4,432,128]{2,1,0:T(8,128)(2,1)}), bf16[4,432,128]{2,1,0:T(8,128)(2,1)S(1)}, u32[]{:S(2)}, u32[]{:S(2)}) async-start(bf16[4,432,128]{2,1,0:T(8,128)(2,1)} %add_convert_fusion), calls=%async_computation.1 | async-start | bytes 884736 | tf_op jit(solution)/shard_map/all_to_all | solution.py:923
  (24 other events, 270.6 us)
where the time goes:
time: 221 us; the launch traced here: 220 us
  waiting for transfers between devices  94.4 us (43%)
  Pallas kernels  76 us (34%)
  starting transfers between devices  29.8 us (13%)
  local copies, waits for them, and re-layouts  13.2 us (6%)
  other arithmetic  5.8 us (3%)
    ppermute x20, waiting for transfers between devices, swap(): return lax.ppermute(value, axis, [(i, i ^ flip) for i in range(count)])  57.2 us
    pallas_call x1, Pallas kernels, local(): pl.pallas_call(functools.partial(backward_kernel, plan), out_shape=[shape...  37.2 us
    pallas_call x1, Pallas kernels, local(): pl.pallas_call(functools.partial(forward_kernel, plan), out_shape=[shape(...  27.9 us
    ppermute x6, waiting for transfers between devices, along(): lax.ppermute(value, 'dp', [(i, (i + 2) % count) for i in range(count)])  26 us
    ppermute x20, starting transfers between devices, swap(): return lax.ppermute(value, axis, [(i, i ^ flip) for i in range(count)])  14.6 us
    unnamed x40, local copies, waits for them, and re-layouts  9.47 us
    ppermute x6, starting transfers between devices, along(): lax.ppermute(value, 'dp', [(i, (i + 2) % count) for i in range(count)])  7.51 us
    all_to_all x1, waiting for transfers between devices, local(): mine = lax.all_to_all(packed, 'seq', 0, 0)  6.37 us
  transfers between devices with their start and end apart: 28, of which 16 were waited for; matrix products, arithmetic and copies ran while one was open for 4% of the time, Pallas kernels for 0%

commit v1 on v0

--- a/solution.py
+++ b/solution.py
@@ -65,6 +65,7 @@
             first = start[i] // PROJ
             last = (min(start[i] + length, IN_SIZE) - 1) // PROJ
             rows.append((first, last - first + 1))
+        self.rows = rows
         self.pure = up(max(n for _, n in rows[:-1]), 16)
         self.edge = up(rows[-1][1], 16)
         self.most_rows = max(n for _, n in rows)
@@ -73,13 +74,6 @@
         self.edge_out = up(edge_out, 8)
         self.edge_at = SLABS * self.edge
         self.small_row = (OUT_END - start[-1]) // LANES
-        self.pads = [self.pure] * self.first_out + [self.edge]
-        self.offsets = [int(v) for v in np.cumsum([0] + self.pads[:-1])]
-        self.depth = int(sum(self.pads))
-        row_map = np.full((1, self.depth), -1, np.int32)
-        for (first, n), at in zip(rows, self.offsets):
-            row_map[0, at : at + n] = np.arange(first, first + n)
-        self.row_map = row_map
         place = np.zeros((count, GROUP), np.int32)
         for i in range(self.first_out, count):
             low = max(start[i] - IN_SIZE, 0) // D // HEAD_DIM
@@ -127,7 +121,7 @@
             held = (head <= high) & (form > 0)
             values.append(jnp.where(held, at, -PAD))
             counts.append(jnp.where(held, rows * OUT_SLABS, 0))
-        values += counts
+        values += counts + [index % GROUP]
         return jnp.stack([jnp.asarray(v, jnp.int32) for v in values])
 
 
@@ -181,12 +175,19 @@
         def get(column):
             return rowbuf[pl.ds(column, depth, stride=ROW_SLABS), :]
 
+        def put(rank, j, slab):
+            out_ref[rank ^ sc[12], j * depth : (j + 1) * depth, :] = slab.astype(BF16)
+
+        for half in range(2):
+            for m in range(OWN_SLABS):
+                cols = [get(12 * half + 4 * m + c) for c in range(4)]
+                for rank in range(GROUP):
+                    slab = join_halves(cols[rank // 2], cols[2 + rank // 2], rank)
+                    put(rank, OWN_SLABS * half + m, slab)
+        rest = [get(24), get(25), jnp.where(lane_iota(depth) < HEADS, get(26), 0.0)]
         for rank in range(GROUP):
-            slabs = [own_slab(get, rank, m) for m in range(OWN_SLABS)]
-            slabs += [own_slab(lambda c: get(12 + c), rank, m) for m in range(OWN_SLABS)]
-            slabs += [get(24), get(25), jnp.where(lane_iota(depth) < HEADS, get(26), 0.0)]
-            for j, slab in enumerate(slabs):
-                out_ref[rank, j * depth : (j + 1) * depth, :] = slab.astype(BF16)
+            for j, slab in enumerate(rest):
+                put(rank, 2 * OWN_SLABS + j, slab)
 
     @pl.when(form == 0)
     def _():
@@ -203,7 +204,7 @@
                 row < sc[8 + rank], flat[pl.ds(sc[4 + rank] + PAD, plan.frame), :], 0.0
             )
             for j in range(OUT_SLABS):
-                out_ref[rank, base + j * rows : base + (j + 1) * rows, :] = frame[
+                out_ref[rank ^ sc[12], base + j * rows : base + (j + 1) * rows, :] = frame[
                     pl.ds(j, rows, stride=OUT_SLABS), :
                 ].astype(BF16)
 
@@ -239,7 +240,7 @@
                 small[at : at + 1, :] = own_slab(lambda c: get(76 + c), rank, m)
                 at += 1
             small[at : at + 1, :] = get(88)
-            out_ref[rank, plan.frame : plan.frame + SMALL, :] = small[...].astype(BF16)
+            out_ref[rank ^ sc[12], plan.frame : plan.frame + SMALL, :] = small[...].astype(BF16)
 
 
 def unpack_kernel(
@@ -251,7 +252,7 @@
     form = sc[0]
 
     def total(at, rows):
-        parts = [blk[rank, at : at + rows, :].astype(F32) for rank in range(GROUP)]
+        parts = [blk[rank ^ sc[12], at : at + rows, :].astype(F32) for rank in range(GROUP)]
         return (parts[0] + parts[1]) + (parts[2] + parts[3])
 
     def weights(depth):
@@ -260,7 +261,7 @@
         def get(base):
             def piece(rank, m):
                 at = (base + m) * depth
-                return blk[rank, at : at + depth, :].astype(F32)
+                return blk[rank ^ sc[12], at : at + depth, :].astype(F32)
 
             return piece
 
@@ -289,7 +290,7 @@
             frame[...] = jnp.zeros_like(frame)
             for j in range(OUT_SLABS):
                 frame[pl.ds(j, count, stride=OUT_SLABS), :] = blk[
-                    rank, base + j * count : base + (j + 1) * count, :
+                    rank ^ sc[12], base + j * count : base + (j + 1) * count, :
                 ].astype(F32)
             row = lax.broadcasted_iota(jnp.int32, (plan.frame, LANES), 0)
             flat[pl.ds(sc[4 + rank] + PAD, plan.frame), :] += jnp.where(
@@ -314,7 +315,7 @@
     @pl.when(sc[3] == 1)
     def _():
         base = PAD + plan.small_row
-        rows = [blk[rank, plan.frame : plan.frame + SMALL, :].astype(F32) for rank in range(GROUP)]
+        rows = [blk[rank ^ sc[12], plan.frame : plan.frame + SMALL, :].astype(F32) for rank in range(GROUP)]
         summed = (rows[0] + rows[1]) + (rows[2] + rows[3])
 
         def get(start):
@@ -468,12 +469,12 @@
     xf[8 : 8 + tokens, :] = proj[:, OWN : OWN + MIXED].astype(F32)
 
 
-def forward_kernel(plan, place, sc, row_map, tok, segr, *refs):
+def forward_kernel(plan, place, sc, tok, segr, *refs):
     dp = plan.dp
     x_in, c_in, w_in = refs[:4], refs[4:8], refs[8 : 8 + dp]
     refs = refs[8 + dp :]
-    (proj, ssd, d_gated, states, sums_ref, w_sf, w_out, small_ref, spread, x_hat, cots) = refs[:11]
-    xs, blocks, w_acc, xf, state, sem = refs[11:]
+    (proj, ssd, d_gated, states, sums_ref, w_in_ref, w_out, small_ref, normed, x_hat, cots) = refs[:11]
+    xs, blocks, w_rows, w_acc, xf, state, sem = refs[11:]
     tokens = xs.shape[0]
     piece = tokens // GROUP
     rank, group = sc[0], sc[1]
@@ -492,19 +493,22 @@
         copy.start()
     for copy in copies:
         copy.wait()
+    w_rows[...] = jnp.zeros_like(w_rows)
 
     def rows_of(i, at, depth):
         for j in range(SLABS):
-            w_sf[pl.ds(at, depth), j * LANES : (j + 1) * LANES] = blocks[
-                i // GROUP, i % GROUP, j * depth : (j + 1) * depth, :
-            ]
+            w_rows[j, pl.ds(at, depth), :] += blocks[
+                i // GROUP, (i % GROUP) ^ rank, j * depth : (j + 1) * depth, :
+            ].astype(F32)
 
     def pure_rows(i, carry):
-        rows_of(i, pl.multiple_of(i * plan.pure, plan.pure), plan.pure)
+        rows_of(i, (i * plan.length) // PROJ, plan.pure)
         return carry
 
     lax.fori_loop(0, plan.first_out, pure_rows, 0)
-    rows_of(plan.first_out, plan.offsets[-1], plan.edge)
+    rows_of(plan.first_out, plan.rows[-1][0], plan.edge)
+    for j in range(SLABS):
+        w_in_ref[:, j * LANES : (j + 1) * LANES] = w_rows[j, 0:D, :].astype(BF16)
     w_acc[...] = jnp.zeros_like(w_acc)
     for i in range(plan.first_out, plan.count):
         rows, base = (plan.edge_out, plan.edge_at) if i == plan.first_out else (plan.frame_rows, 0)
@@ -513,17 +517,14 @@
             at = pl.multiple_of(at, HEAD_DIM)
         for j in range(OUT_SLABS):
             w_acc[j, pl.ds(at, rows), :] += blocks[
-                i // GROUP, i % GROUP, base + j * rows : base + (j + 1) * rows, :
+                i // GROUP, (i % GROUP) ^ rank, base + j * rows : base + (j + 1) * rows, :
             ].astype(F32)
     for j in range(OUT_SLABS):
         w_out[:, j * LANES : (j + 1) * LANES] = w_acc[j, 0:OWN, :].astype(BF16)
-    small = blocks[dp - 1, GROUP - 1, plan.frame : plan.frame + SMALL, :].astype(F32)
+    small = blocks[dp - 1, (GROUP - 1) ^ rank, plan.frame : plan.frame + SMALL, :].astype(F32)
     small_ref[...] = small
     sm = Small(small, rank)
     norm_gain = small_rows(small, 25, OUT_SLABS)
-    chosen = (
-        lax.broadcasted_iota(jnp.int32, (D, plan.depth), 0) == row_map[...]
-    ).astype(BF16)
 
     def tile(t, carry):
         at = pl.ds(pl.multiple_of(t * 256, 256), 256)
@@ -531,9 +532,9 @@
         scale = lax.rsqrt(jnp.sum(x * x, axis=1, keepdims=True) * (1.0 / D) + NORM_EPS)
         unit = x * scale
         x_hat[at, :] = unit.astype(BF16)
-        wide = mm((unit * norm_gain).astype(BF16), chosen).astype(BF16)
-        spread[at, :] = wide
-        proj[at, :] = mm(wide, w_sf[...]).astype(BF16)
+        scaled = (unit * norm_gain).astype(BF16)
+        normed[at, :] = scaled
+        proj[at, :] = mm(scaled, w_in_ref[...]).astype(BF16)
         d_gated[at, :] = mm_nt(cots[at, :], w_out[...])
         return carry
 
@@ -570,13 +571,12 @@
 
 
 def backward_kernel(
-    plan, place, sc, row_map, tok, segr, sums_ref, proj, ssd, d_gated, states, w_sf, w_out,
-    small_ref, spread, x_hat, cots, *refs
+    plan, place, sc, tok, segr, sums_ref, proj, ssd, d_gated, states, w_in, w_out, small_ref, normed, x_hat, cots, *refs
 ):
     dp = plan.dp
     blocks_out, act_out, back_out = refs[:dp], refs[dp], refs[dp + 1]
     (blocks, xf, dcf, adjoint, gated, dn, colbuf, acc_gg, acc_skip, acc_conv, acc_head, acc_ng,
-     wide_out, sem) = refs[dp + 2 :]
+     wide_in, wide_out, sem) = refs[dp + 2 :]
     tokens = proj.shape[0]
     piece = tokens // GROUP
     rank, group = sc[0], sc[1]
@@ -666,16 +666,12 @@
         return carry
 
     lax.fori_loop(0, chunks, chunk, 0)
-    chosen = (
-        lax.broadcasted_iota(jnp.int32, (D, plan.depth), 0) == row_map[...]
-    ).astype(BF16)
 
     for token_group in range(GROUP):
         rel = token_group ^ rank
         at = slice(token_group * piece, (token_group + 1) * piece)
         act_out[lax.rem(rel, 2), rel // 2] = mm(gated[at, :], w_out[...]).astype(BF16)
-        wide = mm_nt(dn[at, :], w_sf[...]).astype(BF16)
-        d_normed = mm_nt(wide, chosen)
+        d_normed = mm_nt(dn[at, :], w_in[...])
         back_out[lax.rem(rel, 2), rel // 2] = d_normed.astype(BF16)
         acc_ng[...] += fold(d_normed * x_hat[at, :].astype(F32))
 
@@ -685,17 +681,24 @@
         to = i // GROUP
         return lax.rem(to // 2 + line - group // 2, line) * 2 + (lax.rem(to + group, 2))
 
-    span = SLABS if plan.depth <= 2048 else OWN_SLABS
-    for first in range(0, SLABS, span):
-        grad_in = mm_tn(spread[...], dn[:, first * LANES : (first + span) * LANES])
-        for i in range(plan.first_out + 1):
-            depth, at = plan.pads[i], plan.offsets[i]
-            to = slot(i)
-            for j in range(span):
-                base = (first + j) * depth
-                blocks[to, i % GROUP, base : base + depth, :] = grad_in[
-                    at : at + depth, j * LANES : (j + 1) * LANES
-                ].astype(BF16)
+    grad_in = mm_tn(normed[...], dn[...])
+    for j in range(SLABS):
+        wide_in[j, 0:D, :] = grad_in[:, j * LANES : (j + 1) * LANES]
+        wide_in[j, D:, :] = jnp.zeros((plan.pure, LANES), F32)
+
+    def rows_of(i, at, depth):
+        to = slot(i)
+        for j in range(SLABS):
+            blocks[to, (i % GROUP) ^ rank, j * depth : (j + 1) * depth, :] = wide_in[
+                j, pl.ds(at, depth), :
+            ].astype(BF16)
+
+    def pure_rows(i, carry):
+        rows_of(i, (i * plan.length) // PROJ, plan.pure)
+        return carry
+
+    lax.fori_loop(0, plan.first_out, pure_rows, 0)
+    rows_of(plan.first_out, plan.rows[-1][0], plan.edge)
     grad_out = mm_tn(gated[...], cots[...])
     for j in range(OUT_SLABS):
         wide_out[j, 0:OWN, :] = grad_out[:, j * LANES : (j + 1) * LANES]
@@ -707,7 +710,7 @@
             at = pl.multiple_of(at, HEAD_DIM)
         to = slot(i)
         for j in range(OUT_SLABS):
-            blocks[to, i % GROUP, base + j * rows : base + (j + 1) * rows, :] = wide_out[
+            blocks[to, (i % GROUP) ^ rank, base + j * rows : base + (j + 1) * rows, :] = wide_out[
                 j, pl.ds(at, rows), :
             ].astype(BF16)
     tail = []
@@ -726,7 +729,7 @@
     vec = vec + pltpu.roll(jnp.where(heads, rate, 0.0), rank + HEADS, 1)
     vec = vec + pltpu.roll(jnp.where(heads, skip, 0.0), rank + 2 * HEADS, 1)
     tail += [vec, jnp.zeros((SMALL - len(tail) - 1, LANES), F32)]
-    blocks[slot(plan.count - 1), GROUP - 1, plan.frame : plan.frame + SMALL, :] = jnp.concatenate(
+    blocks[slot(plan.count - 1), (GROUP - 1) ^ rank, plan.frame : plan.frame + SMALL, :] = jnp.concatenate(
         tail, axis=0
     ).astype(BF16)
     copies = [
@@ -777,6 +780,10 @@
     across = swap(value, "seq", 2)
     close = swap(value, "seq", 1)
     return [value, close, across, swap(across, "seq", 1)]
+
+
+def exchange(value):
+    return jnp.stack([value[0]] + [swap(value[r], "seq", r) for r in range(1, GROUP)])
 
 
 def sum_pieces(value):
@@ -800,7 +807,6 @@
     where = plan.scalars(group * seq + rank)
     sc = jnp.stack([rank, group]).astype(jnp.int32)
     place = jnp.asarray(plan.place.reshape(-1))
-    row_map = jnp.asarray(plan.row_map)
 
     flat_params = params.reshape(sublanes, LANES)
     packed = pl.pallas_call(
@@ -820,7 +826,7 @@
     x_pieces = pieces_of(inputs[0])
     cot = out_grad[0].astype(BF16)
     c_pieces = pieces_of(cot)
-    mine = lax.all_to_all(packed, "seq", 0, 0)
+    mine = exchange(packed)
     weights = [mine, swap(mine, "dp", 1)]
     ring = mine
     for _ in range(1, line):
@@ -845,8 +851,7 @@
     tok = jnp.pad(jnp.stack(columns, axis=1), ((0, 8), (0, LANES - len(columns))))
     segr = by_chunk.astype(F32)
 
-    depth = plan.depth
-    limit = 38 * MIB if depth <= 2048 else 63 * MIB
+    limit = 38 * MIB if dp <= 8 else 63 * MIB
     forward = pl.pallas_call(
         functools.partial(forward_kernel, plan),
         out_shape=[
@@ -855,19 +860,20 @@
             shape((tokens, OWN), F32),
             shape((chunks, STATE, OWN), F32),
             shape((8, tokens), F32),
-            shape((depth, WIDE), BF16),
+            shape((D, WIDE), BF16),
             shape((OWN, D), BF16),
             shape((SMALL, LANES), F32),
-            shape((tokens, depth), BF16),
+            shape((tokens, D), BF16),
             shape((tokens, D), BF16),
             shape((tokens, D), BF16),
         ],
-        in_specs=[smem_spec(), smem_spec(), vmem_spec(), vmem_spec(), vmem_spec()]
+        in_specs=[smem_spec(), smem_spec(), vmem_spec(), vmem_spec()]
         + [any_spec()] * (2 * GROUP + dp),
         out_specs=[vmem_spec()] * 11,
         scratch_shapes=[
             pltpu.VMEM((tokens, D), F32),
             pltpu.VMEM((dp, GROUP, block, LANES), BF16),
+            pltpu.VMEM((SLABS, D + plan.pure, LANES), F32),
             pltpu.VMEM((OUT_SLABS, OWN + plan.frame_rows, LANES), F32),
             pltpu.VMEM((tokens + 8, MIXED), F32),
             pltpu.VMEM((STATE, OWN), F32),
@@ -875,16 +881,16 @@
         ],
         name="forward",
         **params_of(8e9, 3e7, limit),
-    )(place, sc, row_map, tok, segr, *x_pieces, *c_pieces, *weights)
-    proj, ssd, d_gated, states, sums, w_sf, w_out, small, spread, x_hat, cots = forward
-    sums = sums + swap(sums, "seq", 1)
-    sums = sums + swap(sums, "seq", 2)
+    )(place, sc, tok, segr, *x_pieces, *c_pieces, *weights)
+    proj, ssd, d_gated, states, sums, w_in, w_out, small, normed, x_hat, cots = forward
+    near, far, both = [swap(sums, "seq", r) for r in range(1, GROUP)]
+    sums = (sums + near) + (far + both)
 
     backward = pl.pallas_call(
         functools.partial(backward_kernel, plan),
         out_shape=[shape((GROUP, block, LANES), BF16)] * dp
         + [shape((2, 2, piece, D), BF16)] * 2,
-        in_specs=[smem_spec(), smem_spec()] + [vmem_spec()] * 14,
+        in_specs=[smem_spec(), smem_spec()] + [vmem_spec()] * 13,
         out_specs=[any_spec()] * dp + [vmem_spec()] * 2,
         scratch_shapes=[
             pltpu.VMEM((dp, GROUP, block, LANES), BF16),
@@ -899,12 +905,13 @@
             pltpu.VMEM((8 * (KERNEL + 1), MIXED), F32),
             pltpu.VMEM((16, LANES), F32),
             pltpu.VMEM((8, D), F32),
+            pltpu.VMEM((SLABS, D + plan.pure, LANES), F32),
             pltpu.VMEM((OUT_SLABS, OWN + plan.frame_rows, LANES), F32),
             pltpu.SemaphoreType.DMA((dp,)),
         ],
         name="backward",
         **params_of(16e9, 4e7, limit),
-    )(place, sc, row_map, tok, segr, sums, proj, ssd, d_gated, states, w_sf, w_out, small, spread,
+    )(place, sc, tok, segr, sums, proj, ssd, d_gated, states, w_in, w_out, small, normed,
       x_hat, cots)
     terms, act_terms, back_terms = backward[:dp], backward[dp], backward[dp + 1]
 
@@ -920,7 +927,7 @@
         moving = along(here if moving is None else joined(here, moving))
     here = column(0)
     reduced = here if moving is None else joined(here, moving)
-    blocks = lax.all_to_all(reduced, "seq", 0, 0)
+    blocks = exchange(reduced)
 
     flat_shape = shape((sublanes, LANES), F32)
     updated = pl.pallas_call(

time: 221 us -> 210 us (0.950)
  Pallas kernels: 76 us -> 68.1 us
  starting transfers between devices: 29.8 us -> 27.2 us
    ppermute x6, waiting for transfers between devices: 26 us -> 37.2 us  [along(): lax.ppermute(value, 'dp', [(i, (i + 2) % count) for i in range(count)])]
    all_to_all x2 -> x0, waiting for transfers between devices: 11.2 us -> none  [the longest x1 6.37 us: local(): mine = lax.all_to_all(packed, 'seq', 0, 0)]
    ppermute x20 -> x27, starting transfers between devices: 14.6 us -> 24.4 us  [swap(): return lax.ppermute(value, axis, [(i, i ^ flip) for i in range(count)])]
    all_to_all x2 -> x0, starting transfers between devices: 7.7 us -> none  [the longest x1 4.24 us: local(): mine = lax.all_to_all(packed, 'seq', 0, 0)]
    ppermute x6, starting transfers between devices: 7.51 us -> 2.89 us  [along(): lax.ppermute(value, 'dp', [(i, (i + 2) % count) for i in range(count)])]
    pallas_call x1, Pallas kernels: 27.9 us -> 24.4 us  [local(): pl.pallas_call(functools.partial(forward_kernel, plan), out_shape=[shape(...]
    pallas_call x1, Pallas kernels: 37.2 us -> 33.7 us  [local(): pl.pallas_call(functools.partial(backward_kernel, plan), out_shape=[shape...]
    ppermute x20 -> x27, waiting for transfers between devices: 57.2 us -> 59.4 us  [swap(): return lax.ppermute(value, axis, [(i, i ^ flip) for i in range(count)])]
  transfers between devices with their start and end apart: 28 -> 33, of which waited for: 16 -> 19; matrix products, arithmetic and copies ran while one was open for 4% -> 3% of each run, Pallas kernels for 0% -> 0%
where the time goes in v1:
time: 210 us; the launch traced here: 209 us
  waiting for transfers between devices  96.6 us (46%)
  Pallas kernels  68.1 us (32%)
  starting transfers between devices  27.2 us (13%)
  local copies, waits for them, and re-layouts  12.5 us (6%)
  other arithmetic  3.63 us (2%)
    ppermute x27, waiting for transfers between devices, swap(): return lax.ppermute(value, axis, [(i, i ^ flip) for i in range(count)])  59.4 us
    ppermute x6, waiting for transfers between devices, along(): lax.ppermute(value, 'dp', [(i, (i + 2) % count) for i in range(count)])  37.2 us
    pallas_call x1, Pallas kernels, local(): pl.pallas_call(functools.partial(backward_kernel, plan), out_shape=[shape...  33.7 us
    pallas_call x1, Pallas kernels, local(): pl.pallas_call(functools.partial(forward_kernel, plan), out_shape=[shape(...  24.4 us
    ppermute x27, starting transfers between devices, swap(): return lax.ppermute(value, axis, [(i, i ^ flip) for i in range(count)])  24.4 us
    unnamed x36, local copies, waits for them, and re-layouts  9.46 us
    pallas_call x1, Pallas kernels, local(): pl.pallas_call(functools.partial(unpack_kernel, plan), out_shape=[flat_sh...  5.83 us
  transfers between devices with their start and end apart: 33, of which 19 were waited for; matrix products, arithmetic and copies ran while one was open for 3% of the time, Pallas kernels for 0%

profile of v1, /device:TPU:0, one launch (start us, length us, event | category | flops | bytes accessed | tf_op | source)
XLA Modules:
  0.0 209.4 jit_solution(4209429731715356332)
XLA Ops:
  2.1 4.2 %pack.1 = bf16[4,432,128]{2,1,0:T(8,128)(2,1)S(1)} custom-call(s32[13]{0:T(128)S(1)} %stack.120.sc, f32[920,128]{1,0:T(8,128)S(1)} %bitcast.104), custom_call_target="tpu_custom_call" | custom-call | flops 1000000 | bytes 2000000 | tf_op jit(solution)/shard_map/pack/pallas_call | solution.py:812
  6.9 2.6 %collective-permute-start.7 = (bf16[432,128]{1,0:T(8,128)(2,1)S(1)}, bf16[432,128]{1,0:T(8,128)(2,1)S(1)}, u32[]{:S(2)}, u32[]{:S(2)}) collective-permute-start(bf16[432,128]{1,0:T(8,128)(2,1)S(1)} %get-tuple-element.64), channel_id=1, source_target_pairs={{0,2},{1,3},{2,0},{3,1},{4,6},{5,7},{6,4},{7,5},{8,10},{9,11},{10,... | collective-permute-start | bytes 331784 | tf_op jit(solution)/shard_map/ppermute | solution.py:771
  11.2 2.1 %collective-permute-done.7 = bf16[432,128]{1,0:T(8,128)(2,1)S(1)} collective-permute-done((bf16[432,128]{1,0:T(8,128)(2,1)S(1)}, bf16[432,128]{1,0:T(8,128)(2,1)S(1)}, u32[]{:S(2)}, u32[]{:S(2)}) %collective-permute-start.7) | collective-permute-done | bytes 110624 | tf_op jit(solution)/shard_map/ppermute | solution.py:771
  13.3 1.9 collective-permute-done.8
  18.8 10.8 %collective-permute-done.10.refs_10_ = bf16[4,432,128]{2,1,0:T(8,128)(2,1)} collective-permute-done((bf16[4,432,128]{2,1,0:T(8,128)(2,1)S(1)}, bf16[4,432,128]{2,1,0:T(8,128)(2,1)}, u32[]{:S(2)}, u32[]{:S(2)}) %collective-permute-start.10) | collective-permute-done | bytes 442400 | tf_op jit(solution)/shard_map/ppermute | solution.py:776
  30.1 1.8 collective-permute-start.9
  31.9 8.8 %collective-permute-done.4.refs_6_ = bf16[256,768]{1,0:T(8,128)(2,1)S(1)} collective-permute-done((bf16[256,768]{1,0:T(8,128)(2,1)S(1)}, bf16[256,768]{1,0:T(8,128)(2,1)S(1)}, u32[]{:S(2)}, u32[]{:S(2)}) %collective-permute-start.4) | collective-permute-done | bytes 393248 | tf_op jit(solution)/shard_map/ppermute | solution.py:771
  45.8 2.5 %collective-permute-start.11 = (bf16[4,432,128]{2,1,0:T(8,128)(2,1)}, bf16[4,432,128]{2,1,0:T(8,128)(2,1)}, u32[]{:S(2)}, u32[]{:S(2)}) collective-permute-start(bf16[4,432,128]{2,1,0:T(8,128)(2,1)} %collective-permute-done.10.refs_10_), channel_id=1, source_target_pairs={{0,4},{4,0},{8,12},{12,8},{16,20},{20,16},{24,28},{28,24},{1,5},{5... | collective-permute-start | bytes 1327112 | tf_op jit(solution)/shard_map/ppermute | solution.py:771
  49.1 7.1 %collective-permute-done.14.refs_14_ = bf16[4,432,128]{2,1,0:T(8,128)(2,1)} collective-permute-done((bf16[4,432,128]{2,1,0:T(8,128)(2,1)}, bf16[4,432,128]{2,1,0:T(8,128)(2,1)}, u32[]{:S(2)}, u32[]{:S(2)}) %collective-permute-start.14) | collective-permute-done | bytes 442400 | tf_op jit(solution)/shard_map/ppermute | solution.py:776
  56.2 2.9 %collective-permute-start.15 = (bf16[4,432,128]{2,1,0:T(8,128)(2,1)}, bf16[4,432,128]{2,1,0:T(8,128)(2,1)}, u32[]{:S(2)}, u32[]{:S(2)}) collective-permute-start(bf16[4,432,128]{2,1,0:T(8,128)(2,1)} %collective-permute-done.14.refs_14_), channel_id=1, source_target_pairs={{0,4},{4,0},{8,12},{12,8},{16,20},{20,16},{24,28},{28,24},{1,5},{5... | collective-permute-start | bytes 1327112 | tf_op jit(solution)/shard_map/ppermute | solution.py:771
  61.7 7.4 %collective-permute-done.13.refs_13_ = bf16[4,432,128]{2,1,0:T(8,128)(2,1)} collective-permute-done((bf16[4,432,128]{2,1,0:T(8,128)(2,1)}, bf16[4,432,128]{2,1,0:T(8,128)(2,1)}, u32[]{:S(2)}, u32[]{:S(2)}) %collective-permute-start.13) | collective-permute-done | bytes 442400 | tf_op jit(solution)/shard_map/ppermute | solution.py:771
  69.1 8.8 %collective-permute-done.15.refs_15_ = bf16[4,432,128]{2,1,0:T(8,128)(2,1)} collective-permute-done((bf16[4,432,128]{2,1,0:T(8,128)(2,1)}, bf16[4,432,128]{2,1,0:T(8,128)(2,1)}, u32[]{:S(2)}, u32[]{:S(2)}) %collective-permute-start.15) | collective-permute-done | bytes 442400 | tf_op jit(solution)/shard_map/ppermute | solution.py:771
  81.9 24.4 %forward.1 = (bf16[1024,1152]{1,0:T(8,128)(2,1)}, f32[1024,384]{1,0:T(8,128)S(1)}, f32[1024,384]{1,0:T(8,128)S(1)}, f32[8,128,384]{2,1,0:T(8,128)S(1)}, f32[8,10...) custom-call(s32[128]{0:T(128)S(1)} %copy-done.13, ...), custom_call_target="tpu_custom_call" | custom-call | flops 8000000000 | bytes 30000000 | tf_op jit(solution)/shard_map/forward/pallas_call | solution.py:855
  106.5 1.9 collective-permute-start.17
  108.5 1.9 collective-permute-done.17
  113.1 33.7 %backward.1 = (bf16[4,432,128]{2,1,0:T(8,128)(2,1)S(1)}, bf16[4,432,128]{2,1,0:T(8,128)(2,1)S(1)}, bf16[4,432,128]{2,1,0:T(8,128)(2,1)S(1)}, bf16[4,432,128]{2,1...) custom-call(s32[128]{0:T(128)S(1)} %copy-done.13, ...), custom_call_target="tpu_custom_call" | custom-call | flops 16000000000 | bytes 40000000 | tf_op jit(solution)/shard_map/backward/pallas_call | solution.py:889
  151.2 8.8 %collective-permute-done.26 = bf16[4,432,128]{2,1,0:T(8,128)(2,1)S(1)} collective-permute-done((bf16[4,432,128]{2,1,0:T(8,128)(2,1)S(1)}, bf16[4,432,128]{2,1,0:T(8,128)(2,1)S(1)}, u32[]{:S(2)}, u32[]{:S(2)}) %collective-permute-start.26) | collective-permute-done | bytes 442400 | tf_op jit(solution)/shard_map/ppermute | solution.py:771
  161.2 8.3 %collective-permute-done.25 = bf16[4,432,128]{2,1,0:T(8,128)(2,1)S(1)} collective-permute-done((bf16[4,432,128]{2,1,0:T(8,128)(2,1)S(1)}, bf16[4,432,128]{2,1,0:T(8,128)(2,1)S(1)}, u32[]{:S(2)}, u32[]{:S(2)}) %collective-permute-start.25) | collective-permute-done | bytes 442400 | tf_op jit(solution)/shard_map/ppermute | solution.py:771
  169.4 3.3 %collective-permute-done.27 = bf16[4,432,128]{2,1,0:T(8,128)(2,1)S(1)} collective-permute-done((bf16[4,432,128]{2,1,0:T(8,128)(2,1)S(1)}, bf16[4,432,128]{2,1,0:T(8,128)(2,1)S(1)}, u32[]{:S(2)}, u32[]{:S(2)}) %collective-permute-start.27) | collective-permute-done | bytes 442400 | tf_op jit(solution)/shard_map/ppermute | solution.py:776
  174.1 4.8 %collective-permute-done.24 = bf16[4,432,128]{2,1,0:T(8,128)(2,1)S(1)} collective-permute-done((bf16[4,432,128]{2,1,0:T(8,128)(2,1)S(1)}, bf16[4,432,128]{2,1,0:T(8,128)(2,1)S(1)}, u32[]{:S(2)}, u32[]{:S(2)}) %collective-permute-start.24) | collective-permute-done | bytes 442400 | tf_op jit(solution)/shard_map/ppermute | solution.py:771
  178.9 5.9 %collective-permute-done.28 = bf16[4,432,128]{2,1,0:T(8,128)(2,1)S(1)} collective-permute-done((bf16[4,432,128]{2,1,0:T(8,128)(2,1)S(1)}, bf16[4,432,128]{2,1,0:T(8,128)(2,1)S(1)}, u32[]{:S(2)}, u32[]{:S(2)}) %collective-permute-start.28) | collective-permute-done | bytes 442400 | tf_op jit(solution)/shard_map/ppermute | solution.py:776
  187.6 8.3 %collective-permute-done.29 = bf16[4,432,128]{2,1,0:T(8,128)(2,1)S(1)} collective-permute-done((bf16[4,432,128]{2,1,0:T(8,128)(2,1)S(1)}, bf16[4,432,128]{2,1,0:T(8,128)(2,1)S(1)}, u32[]{:S(2)}, u32[]{:S(2)}) %collective-permute-start.29) | collective-permute-done | bytes 442400 | tf_op jit(solution)/shard_map/ppermute | solution.py:776
  199.6 2.6 %collective-permute-done.31 = bf16[432,128]{1,0:T(8,128)(2,1)S(1)} collective-permute-done((bf16[432,128]{1,0:T(8,128)(2,1)S(1)}, bf16[432,128]{1,0:T(8,128)(2,1)S(1)}, u32[]{:S(2)}, u32[]{:S(2)}) %collective-permute-start.31) | collective-permute-done | bytes 110624 | tf_op jit(solution)/shard_map/ppermute | solution.py:771
  203.6 5.8 %unpack.1 = (f32[920,128]{1,0:T(8,128)}, f32[920,128]{1,0:T(8,128)}, f32[920,128]{1,0:T(8,128)}, f32[920,128]{1,0:T(8,128)}) custom-call(s32[13]{0:T(128)S(1)} %stack.120.sc, bf16[4,432,128]{2,1,0:T(8,128)(2,1)S(1)} %pad_maximum_fusion.1.blk, f32[920,128]{1,0:T(8,128)S(1)} %bitcast.105, f32[920,128]{1,0:T(8,128)S(1)} %bitcast.106, f32[920,128]{1,0:T(8,128)S(1)} %bitcast.107), custom_call_target="tpu_custom_call" | custom-call | flops 1000000 | bytes 5000000 | tf_op jit(solution)/shard_map/unpack/pallas_call | solution.py:933
  (121 shorter events, 37.4 us)
Async XLA Ops:
  9.5 35.0 %collective-permute-start.1 = (f32[256,768]{1,0:T(8,128)S(1)}, f32[256,768]{1,0:T(8,128)S(1)}, u32[]{:S(2)}, u32[]{:S(2)}) collective-permute-start(f32[256,768]{1,0:T(8,128)S(1)} %bitcast.101), channel_id=1, source_target_pairs={{0,2},{1,3},{2,0},{3,1},{4,6},{5,7},{6,4},{7,5},{8,10},{9,11},{10,... | collective-permute-start | bytes 2359304 | tf_op jit(solution)/shard_map/ppermute | solution.py:771
  15.3 14.3 %collective-permute-start.10 = (bf16[4,432,128]{2,1,0:T(8,128)(2,1)S(1)}, bf16[4,432,128]{2,1,0:T(8,128)(2,1)}, u32[]{:S(2)}, u32[]{:S(2)}) collective-permute-start(bf16[4,432,128]{2,1,0:T(8,128)(2,1)S(1)} %pad_maximum_fusion.refs_8_), channel_id=1, source_target_pairs={{0,8},{4,12},{8,16},{12,20},{16,24},{20,28},{24,0},{28,4},{1,9},{5... | collective-permute-start | bytes 1327112 | tf_op jit(solution)/shard_map/ppermute | solution.py:776
  17.0 23.7 %collective-permute-start.4 = (bf16[256,768]{1,0:T(8,128)(2,1)S(1)}, bf16[256,768]{1,0:T(8,128)(2,1)S(1)}, u32[]{:S(2)}, u32[]{:S(2)}) collective-permute-start(bf16[256,768]{1,0:T(8,128)(2,1)S(1)} %bitcast_convert_fusion.refs_4_), channel_id=1, source_target_pairs={{0,2},{1,3},{2,0},{3,1},{4,6},{5,7},{6,4},{7,5},{8,10},{9,11},{10,... | collective-permute-start | bytes 1179656 | tf_op jit(solution)/shard_map/ppermute | solution.py:771
  18.5 25.0 %collective-permute-start.3 = (bf16[256,768]{1,0:T(8,128)(2,1)S(1)}, bf16[256,768]{1,0:T(8,128)(2,1)S(1)}, u32[]{:S(2)}, u32[]{:S(2)}) collective-permute-start(bf16[256,768]{1,0:T(8,128)(2,1)S(1)} %bitcast_convert_fusion.refs_4_), channel_id=1, source_target_pairs={{0,1},{1,0},{2,3},{3,2},{4,5},{5,4},{6,7},{7,6},{8,9},{9,8},{10,11... | collective-permute-start | bytes 1179656 | tf_op jit(solution)/shard_map/ppermute | solution.py:771
  29.6 13.6 %collective-permute-start.12 = (bf16[4,432,128]{2,1,0:T(8,128)(2,1)}, bf16[4,432,128]{2,1,0:T(8,128)(2,1)}, u32[]{:S(2)}, u32[]{:S(2)}) collective-permute-start(bf16[4,432,128]{2,1,0:T(8,128)(2,1)} %collective-permute-done.10.refs_10_), channel_id=1, source_target_pairs={{0,8},{4,12},{8,16},{12,20},{16,24},{20,28},{24,0},{28,4},{1,9},{5... | collective-permute-start | bytes 1327112 | tf_op jit(solution)/shard_map/ppermute | solution.py:776
  30.1 14.9 %collective-permute-start.9 = (bf16[4,432,128]{2,1,0:T(8,128)(2,1)S(1)}, bf16[4,432,128]{2,1,0:T(8,128)(2,1)S(1)}, u32[]{:S(2)}, u32[]{:S(2)}) collective-permute-start(bf16[4,432,128]{2,1,0:T(8,128)(2,1)S(1)} %pad_maximum_fusion.refs_8_), channel_id=1, source_target_pairs={{0,4},{4,0},{8,12},{12,8},{16,20},{20,16},{24,28},{28,24},{1,5},{5... | collective-permute-start | bytes 1327112 | tf_op jit(solution)/shard_map/ppermute | solution.py:771
  40.7 7.6 %collective-permute-start.5 = (bf16[256,768]{1,0:T(8,128)(2,1)S(1)}, bf16[256,768]{1,0:T(8,128)(2,1)S(1)}, u32[]{:S(2)}, u32[]{:S(2)}) collective-permute-start(bf16[256,768]{1,0:T(8,128)(2,1)S(1)} %collective-permute-done.4.refs_6_), channel_id=1, source_target_pairs={{0,1},{1,0},{2,3},{3,2},{4,5},{5,4},{6,7},{7,6},{8,9},{9,8},{10,11... | collective-permute-start | bytes 1179656 | tf_op jit(solution)/shard_map/ppermute | solution.py:771
  43.2 12.9 %collective-permute-start.14 = (bf16[4,432,128]{2,1,0:T(8,128)(2,1)}, bf16[4,432,128]{2,1,0:T(8,128)(2,1)}, u32[]{:S(2)}, u32[]{:S(2)}) collective-permute-start(bf16[4,432,128]{2,1,0:T(8,128)(2,1)} %collective-permute-done.12.refs_12_), channel_id=1, source_target_pairs={{0,8},{4,12},{8,16},{12,20},{16,24},{20,28},{24,0},{28,4},{1,9},{5... | collective-permute-start | bytes 1327112 | tf_op jit(solution)/shard_map/ppermute | solution.py:776
  44.3 17.5 %collective-permute-start = (f32[256,768]{1,0:T(8,128)S(1)}, f32[256,768]{1,0:T(8,128)S(1)}, u32[]{:S(2)}, u32[]{:S(2)}) collective-permute-start(f32[256,768]{1,0:T(8,128)S(1)} %bitcast.102), channel_id=1, source_target_pairs={{0,1},{1,0},{2,3},{3,2},{4,5},{5,4},{6,7},{7,6},{8,9},{9,8},{10,11... | collective-permute-start | bytes 2359304 | tf_op jit(solution)/shard_map/ppermute | solution.py:771
  44.5 24.7 %collective-permute-start.2 = (f32[256,768]{1,0:T(8,128)S(1)}, f32[256,768]{1,0:T(8,128)}, u32[]{:S(2)}, u32[]{:S(2)}) collective-permute-start(f32[256,768]{1,0:T(8,128)S(1)} %collective-permute-done.1.refs_2_), channel_id=1, source_target_pairs={{0,1},{1,0},{2,3},{3,2},{4,5},{5,4},{6,7},{7,6},{8,9},{9,8},{10,11... | collective-permute-start | bytes 2359304 | tf_op jit(solution)/shard_map/ppermute | solution.py:771
  45.8 15.9 %collective-permute-start.11 = (bf16[4,432,128]{2,1,0:T(8,128)(2,1)}, bf16[4,432,128]{2,1,0:T(8,128)(2,1)}, u32[]{:S(2)}, u32[]{:S(2)}) collective-permute-start(bf16[4,432,128]{2,1,0:T(8,128)(2,1)} %collective-permute-done.10.refs_10_), channel_id=1, source_target_pairs={{0,4},{4,0},{8,12},{12,8},{16,20},{20,16},{24,28},{28,24},{1,5},{5... | collective-permute-start | bytes 1327112 | tf_op jit(solution)/shard_map/ppermute | solution.py:771
  49.1 20.1 %collective-permute-start.13 = (bf16[4,432,128]{2,1,0:T(8,128)(2,1)}, bf16[4,432,128]{2,1,0:T(8,128)(2,1)}, u32[]{:S(2)}, u32[]{:S(2)}) collective-permute-start(bf16[4,432,128]{2,1,0:T(8,128)(2,1)} %collective-permute-done.12.refs_12_), channel_id=1, source_target_pairs={{0,4},{4,0},{8,12},{12,8},{16,20},{20,16},{24,28},{28,24},{1,5},{5... | collective-permute-start | bytes 1327112 | tf_op jit(solution)/shard_map/ppermute | solution.py:771
  56.2 21.8 %collective-permute-start.15 = (bf16[4,432,128]{2,1,0:T(8,128)(2,1)}, bf16[4,432,128]{2,1,0:T(8,128)(2,1)}, u32[]{:S(2)}, u32[]{:S(2)}) collective-permute-start(bf16[4,432,128]{2,1,0:T(8,128)(2,1)} %collective-permute-done.14.refs_14_), channel_id=1, source_target_pairs={{0,4},{4,0},{8,12},{12,8},{16,20},{20,16},{24,28},{28,24},{1,5},{5... | collective-permute-start | bytes 1327112 | tf_op jit(solution)/shard_map/ppermute | solution.py:771
  146.8 13.1 %collective-permute-start.26 = (bf16[4,432,128]{2,1,0:T(8,128)(2,1)S(1)}, bf16[4,432,128]{2,1,0:T(8,128)(2,1)S(1)}, u32[]{:S(2)}, u32[]{:S(2)}) collective-permute-start(bf16[4,432,128]{2,1,0:T(8,128)(2,1)S(1)} %get-tuple-element.51), channel_id=1, source_target_pairs={{0,4},{4,0},{8,12},{12,8},{16,20},{20,16},{24,28},{28,24},{1,5},{5... | collective-permute-start | bytes 1327112 | tf_op jit(solution)/shard_map/ppermute | solution.py:771
  148.5 12.4 %collective-permute-start.21 = (bf16[2,256,768]{2,1,0:T(8,128)(2,1)S(1)}, bf16[2,256,768]{2,1,0:T(8,128)(2,1)S(1)}, u32[]{:S(2)}, u32[]{:S(2)}) collective-permute-start(bf16[2,256,768]{2,1,0:T(8,128)(2,1)S(1)} %slice_bitcast_fusion), channel_id=1, source_target_pairs={{0,1},{1,0},{2,3},{3,2},{4,5},{5,4},{6,7},{7,6},{8,9},{9,8},{10,11... | collective-permute-start | bytes 2359304 | tf_op jit(solution)/shard_map/ppermute | solution.py:771
  148.6 20.8 %collective-permute-start.25 = (bf16[4,432,128]{2,1,0:T(8,128)(2,1)S(1)}, bf16[4,432,128]{2,1,0:T(8,128)(2,1)S(1)}, u32[]{:S(2)}, u32[]{:S(2)}) collective-permute-start(bf16[4,432,128]{2,1,0:T(8,128)(2,1)S(1)} %get-tuple-element.49), channel_id=1, source_target_pairs={{0,4},{4,0},{8,12},{12,8},{16,20},{20,16},{24,28},{28,24},{1,5},{5... | collective-permute-start | bytes 1327112 | tf_op jit(solution)/shard_map/ppermute | solution.py:771
  149.2 29.8 %collective-permute-start.24 = (bf16[4,432,128]{2,1,0:T(8,128)(2,1)S(1)}, bf16[4,432,128]{2,1,0:T(8,128)(2,1)S(1)}, u32[]{:S(2)}, u32[]{:S(2)}) collective-permute-start(bf16[4,432,128]{2,1,0:T(8,128)(2,1)S(1)} %get-tuple-element.47), channel_id=1, source_target_pairs={{0,4},{4,0},{8,12},{12,8},{16,20},{20,16},{24,28},{28,24},{1,5},{5... | collective-permute-start | bytes 1327112 | tf_op jit(solution)/shard_map/ppermute | solution.py:771
  150.7 36.9 %collective-permute-start.23 = (bf16[4,432,128]{2,1,0:T(8,128)(2,1)S(1)}, bf16[4,432,128]{2,1,0:T(8,128)(2,1)S(1)}, u32[]{:S(2)}, u32[]{:S(2)}) collective-permute-start(bf16[4,432,128]{2,1,0:T(8,128)(2,1)S(1)} %get-tuple-element.45), channel_id=1, source_target_pairs={{0,4},{4,0},{8,12},{12,8},{16,20},{20,16},{24,28},{28,24},{1,5},{5... | collective-permute-start | bytes 1327112 | tf_op jit(solution)/shard_map/ppermute | solution.py:771
  160.1 12.7 %collective-permute-start.27 = (bf16[4,432,128]{2,1,0:T(8,128)(2,1)S(1)}, bf16[4,432,128]{2,1,0:T(8,128)(2,1)S(1)}, u32[]{:S(2)}, u32[]{:S(2)}) collective-permute-start(bf16[4,432,128]{2,1,0:T(8,128)(2,1)S(1)} %add_convert_fusion.3), channel_id=1, source_target_pairs={{0,8},{4,12},{8,16},{12,20},{16,24},{20,28},{24,0},{28,4},{1,9},{5... | collective-permute-start | bytes 1327112 | tf_op jit(solution)/shard_map/ppermute | solution.py:776
  160.9 13.0 %collective-permute-start.19 = (bf16[2,256,768]{2,1,0:T(8,128)(2,1)S(1)}, bf16[2,256,768]{2,1,0:T(8,128)(2,1)S(1)}, u32[]{:S(2)}, u32[]{:S(2)}) collective-permute-start(bf16[2,256,768]{2,1,0:T(8,128)(2,1)S(1)} %slice_bitcast_fusion.1), channel_id=1, source_target_pairs={{0,1},{1,0},{2,3},{3,2},{4,5},{5,4},{6,7},{7,6},{8,9},{9,8},{10,11... | collective-permute-start | bytes 2359304 | tf_op jit(solution)/shard_map/ppermute | solution.py:771
  172.9 11.8 %collective-permute-start.28 = (bf16[4,432,128]{2,1,0:T(8,128)(2,1)S(1)}, bf16[4,432,128]{2,1,0:T(8,128)(2,1)S(1)}, u32[]{:S(2)}, u32[]{:S(2)}) collective-permute-start(bf16[4,432,128]{2,1,0:T(8,128)(2,1)S(1)} %add_convert_fusion.2), channel_id=1, source_target_pairs={{0,8},{4,12},{8,16},{12,20},{16,24},{20,28},{24,0},{28,4},{1,9},{5... | collective-permute-start | bytes 1327112 | tf_op jit(solution)/shard_map/ppermute | solution.py:776
  173.0 12.8 %collective-permute-start.22 = (bf16[256,768]{1,0:T(8,128)(2,1)S(1)}, bf16[256,768]{1,0:T(8,128)(2,1)S(1)}, u32[]{:S(2)}, u32[]{:S(2)}) collective-permute-start(bf16[256,768]{1,0:T(8,128)(2,1)S(1)} %slice_bitcast_fusion.2), channel_id=1, source_target_pairs={{0,2},{1,3},{2,0},{3,1},{4,6},{5,7},{6,4},{7,5},{8,10},{9,11},{10,... | collective-permute-start | bytes 1179656 | tf_op jit(solution)/shard_map/ppermute | solution.py:771
  184.9 11.0 %collective-permute-start.29 = (bf16[4,432,128]{2,1,0:T(8,128)(2,1)S(1)}, bf16[4,432,128]{2,1,0:T(8,128)(2,1)S(1)}, u32[]{:S(2)}, u32[]{:S(2)}) collective-permute-start(bf16[4,432,128]{2,1,0:T(8,128)(2,1)S(1)} %add_convert_fusion.1), channel_id=1, source_target_pairs={{0,8},{4,12},{8,16},{12,20},{16,24},{20,28},{24,0},{28,4},{1,9},{5... | collective-permute-start | bytes 1327112 | tf_op jit(solution)/shard_map/ppermute | solution.py:776
  185.0 13.0 %collective-permute-start.20 = (bf16[256,768]{1,0:T(8,128)(2,1)S(1)}, bf16[256,768]{1,0:T(8,128)(2,1)S(1)}, u32[]{:S(2)}, u32[]{:S(2)}) collective-permute-start(bf16[256,768]{1,0:T(8,128)(2,1)S(1)} %slice_bitcast_fusion.4), channel_id=1, source_target_pairs={{0,2},{1,3},{2,0},{3,1},{4,6},{5,7},{6,4},{7,5},{8,10},{9,11},{10,... | collective-permute-start | bytes 1179656 | tf_op jit(solution)/shard_map/ppermute | solution.py:771
  (27 other events, 182.2 us)
